TPU v7x, 128 devices: a whole 4x4x4 slice. The times are simulated.
128 devices in a mesh: gx: 8 (over y, core), gy: 16 (over x, z).
Axes of the slice: x: 4, y: 4, z: 4, core: 2. Of those that a mesh axis runs over, the one named last changes fastest.
Arguments:
- log_perm: float32 [1, 32, 256, 4096], P(None, None, 'gx', 'gy'), may hold values from -4 to 4
- source: float32 [1, 32, 256, 4096], P(None, None, 'gx', 'gy'), may hold values from -24 to 24
Outputs:
- pressure: float32 [1, 32, 256, 4096], P(None, None, 'gx', 'gy')
- residual: float32 [1, 32, 256, 4096], P(None, None, 'gx', 'gy')
- flux_east: float32 [1, 32, 256, 4096], P(None, None, 'gx', 'gy')
- flux_north: float32 [1, 32, 256, 4096], P(None, None, 'gx', 'gy')
All inputs are finite; a program needn't handle non-finite values.
Results may differ from a plain program's by a relative error of at most 0.0003.
Values sent between devices are 32-bit elements; how exact they have to be, the bound alone decides.
A program may use at most 128 MiB of HBM per device.

v0:
```python
import jax
import jax.numpy as jnp
from jax import lax
from jax.sharding import PartitionSpec as P

OUTER = 2


exact_mode = lax.Precision.HIGHEST


def padded(cells, sides, width):
    for axis, dim in sides:
        count = lax.axis_size(axis)
        ends = count - 1
        head = lax.slice_in_dim(cells, 0, width, axis=dim)
        tail = lax.slice_in_dim(cells, cells.shape[dim] - width, cells.shape[dim], axis=dim)
        cells = jnp.concatenate(
            [
                lax.ppermute(tail, axis, [(i, (i + 1) % count) for i in range(ends)]),
                cells,
                lax.ppermute(head, axis, [((i + 1) % count, i) for i in range(ends)]),
            ],
            axis=dim,
        )
    return cells


def harmonic(first_perm, second_perm):
    return 2.0 * first_perm * second_perm / (first_perm + second_perm)


def apply_region(field_in, transmit, margin_out):
    trans_x, trans_y, trans_z = transmit
    count_rows = field_in.shape[-2] - 2
    count_cols = field_in.shape[-1] - 2
    offset = 2 - margin_out
    row_hi = slice(offset, offset + count_rows)
    row_lo = slice(offset - 1, offset - 1 + count_rows)
    col_hi = slice(offset, offset + count_cols)
    col_lo = slice(offset - 1, offset - 1 + count_cols)
    center = field_in[..., 1:-1, 1:-1]
    depth_pad = [(0, 0)] * (center.ndim - 3) + [(1, 1), (0, 0), (0, 0)]
    vertical = jnp.pad(center, depth_pad)
    result = trans_x[..., row_hi, col_hi] * (center - field_in[..., 2:, 1:-1]) + trans_x[
        ..., row_lo, col_hi
    ] * (center - field_in[..., :-2, 1:-1])
    result = (
        result
        + trans_y[..., row_hi, col_hi] * (center - field_in[..., 1:-1, 2:])
        + trans_y[..., row_hi, col_lo] * (center - field_in[..., 1:-1, :-2])
    )
    upper_face = trans_z[..., 1:, row_hi, col_hi]
    lower_face = trans_z[..., :-1, row_hi, col_hi]
    result = (
        result
        + upper_face * (center - vertical[..., 2:, :, :])
        + lower_face * (center - vertical[..., :-2, :, :])
    )
    return result


def recurrence(gram_matrix):
    batch_count = gram_matrix.shape[0]
    identity = jnp.eye(5, dtype=jnp.float32)
    direc_coef = jnp.broadcast_to(identity[0], (batch_count, 5))
    resid_coef = jnp.broadcast_to(identity[3], (batch_count, 5))
    sol_coef = jnp.zeros((batch_count, 5), jnp.float32)
    zero_col = jnp.zeros((batch_count,), jnp.float32)

    def quadratic(left_coef, right_coef):
        return jnp.einsum("si,sij,sj->s", left_coef, gram_matrix, right_coef, precision=exact_mode)

    for inner_turn in range(2):
        images = jnp.stack(
            [zero_col, direc_coef[:, 0], direc_coef[:, 1], zero_col, direc_coef[:, 3]], axis=1
        )
        rho_old = quadratic(resid_coef, resid_coef)
        step_size = (rho_old / quadratic(direc_coef, images))[:, None]
        sol_coef = sol_coef + step_size * direc_coef
        resid_coef = resid_coef - step_size * images
        ratio_new = (quadratic(resid_coef, resid_coef) / rho_old)[:, None]
        direc_coef = resid_coef + ratio_new * direc_coef
    return (sol_coef, resid_coef, direc_coef)


def combine(coef_in, basis):
    return jnp.einsum("si,iszxy->szxy", coef_in, basis, precision=exact_mode)


def on_device(log_perm, source):
    local_rows = log_perm.shape[2]
    local_cols = log_perm.shape[3]
    wide_log = padded(log_perm, (("gx", 2), ("gy", 3)), 2)
    wide_perm = jnp.exp(wide_log)
    trans_x = harmonic(wide_perm[..., 1:, :], wide_perm[..., :-1, :])
    trans_y = harmonic(wide_perm[..., 1:], wide_perm[..., :-1])
    trans_z = jnp.pad(
        harmonic(wide_perm[:, 1:], wide_perm[:, :-1]), ((0, 0), (1, 1), (0, 0), (0, 0))
    )
    transmit = (trans_x, trans_y, trans_z)
    pressure = jnp.zeros_like(source)
    resid_field = source
    direc_field = source
    for outer_turn in range(OUTER):
        stacked = jnp.stack([direc_field, resid_field])
        narrow_rim = padded(stacked, (("gx", 3), ("gy", 4)), 1)
        first_pass = apply_region(narrow_rim, transmit, 0)
        power_one = first_pass[0]
        resid_image = first_pass[1]
        power_cycle = padded(power_one, (("gx", 2), ("gy", 3)), 1)
        power_two = apply_region(power_cycle, transmit, 0)
        basis = jnp.stack([direc_field, power_one, power_two, resid_field, resid_image])
        local_gram = jnp.einsum("iszxy,jszxy->sij", basis, basis, precision=exact_mode)
        gram_matrix = lax.psum(local_gram, ("gx", "gy"))
        sol_coef, resid_coef, direc_coef = recurrence(gram_matrix)
        pressure = pressure + combine(sol_coef, basis)
        resid_field = combine(resid_coef, basis)
        direc_field = combine(direc_coef, basis)
    pressure_rim = padded(pressure, (("gx", 2), ("gy", 3)), 1)
    residual = source - apply_region(pressure_rim, transmit, 0)
    flux_east = trans_x[..., 2 : 2 + local_rows, 2 : 2 + local_cols] * (
        pressure - pressure_rim[..., 2:, 1:-1]
    )
    flux_north = trans_y[..., 2 : 2 + local_rows, 2 : 2 + local_cols] * (
        pressure - pressure_rim[..., 1:-1, 2:]
    )
    return (pressure, residual, flux_east, flux_north)


def solution(mesh):
    placed = (P(None, None, "gx", "gy"), P(None, None, "gx", "gy"))
    return jax.shard_map(
        on_device,
        mesh=mesh,
        in_specs=placed,
        out_specs=(
            P(None, None, "gx", "gy"),
            P(None, None, "gx", "gy"),
            P(None, None, "gx", "gy"),
            P(None, None, "gx", "gy"),
        ),
        check_vma=False,
    )
```

profile of v0, /device:TPU:12, one launch (start us, length us, event | category | flops | bytes accessed | tf_op | source)
XLA Modules:
  0.0 471.1 jit_solution(8709827635814640932)
XLA Ops:
  1.9 1.9 collective-permute-start
  3.8 3.6 collective-permute-start.1
  8.8 1.9 collective-permute-start.4
  10.7 2.4 collective-permute-start.5
  16.9 3.8 collective-permute-start.2
  21.0 4.1 collective-permute-start.3
  28.8 3.8 collective-permute-start.6
  33.1 2.0 collective-permute-start.7
  38.4 2.7 collective-permute-done.7
  44.3 2.1 maximum_exponential_fusion
  54.4 3.3 fusion.15
  59.2 1.9 collective-permute-start.8
  61.1 2.4 collective-permute-start.9
  63.6 2.8 collective-permute-done.9
  69.2 3.4 collective-permute-start.10
  74.0 2.5 collective-permute-start.11
  78.2 3.5 collective-permute-done.11
  82.9 10.7 %fusion.66 = f32[5,1,32,32,256]{4,3,2,1,0:T(8,128)} fusion(f32[5,1,32,32,256]{4,3,2,1,0:T(8,128)} %get-tuple-element.24, f32[1,32,32,256]{3,2,1,0:T(8,128)} %copy-done.6, f32[1,32,34,1]{3,2,1,0:T(8,128)} %copy.73, f32[1,32,1,256]{3,2,1,0:T(1,128)S(1)} %collective-permute-done.8, f32[1,32,1,256]{3,2,1,0:T(1,128)S(1)} %collective-permute-done.9, ...), kind=kLoop, calls=%fused_computation.127 | loop fusion | flops 6553600 | bytes 9572352
  96.7 28.0 %fusion.46 = f32[5,5]{1,0:T(8,128)S(1)} fusion(f32[5,32,32,256]{3,2,1,0:T(8,128)} %bitcast.11), kind=kOutput, calls=%fused_computation.96 | convolution fusion | flops 78643200 | bytes 5242980 | tf_op jit(solution)/shard_map/iszxy,jszxy->sij/dot_general | solution.py:114
  125.3 62.2 %psum.14 = f32[5,5]{1,0:T(8,128)S(1)} all-reduce(f32[5,5]{1,0:T(8,128)S(1)} %fusion.46), channel_id=1, replica_groups=mesh['gx'=8,'gy'=16] {'gx','gy'}, use_global_device_ids=true, to_apply=%region_0.1 | all-reduce | flops 25 | bytes 200 | tf_op jit(solution)/shard_map/psum | solution.py:115
  197.8 14.8 %fusion = f32[1,32,32,256]{3,0,2,1:T(1,128)} fusion(f32[5,32,32,256]{3,2,1,0:T(8,128)} %bitcast.11, f32[1,5]{1,0:T(1,128)S(1)} %multiply_subtract_fusion.2, f32[]{:T(128)S(6)} %div.42, f32[1,1]{1,0:T(1,128)} %slice.361, f32[1,1]{1,0:T(1,128)} %constant.1.clone.1, f32[1,2]{1,0:T(1,128)S(1)} %bitcast.211), kind=kOutput, calls=%fused_computation | convolution fusion | flops 15728665 | bytes 6291496 | tf_op jit(solution)/shard_map/si,iszxy->szxy/dot_general | solution.py:88
  213.9 14.4 %fusion.2 = f32[1,32,32,256]{3,0,2,1:T(1,128)S(1)} fusion(f32[5,32,32,256]{3,2,1,0:T(8,128)} %bitcast.11, f32[1,5]{1,0:T(1,128)S(1)} %multiply_add_fusion.1, f32[]{:T(128)S(6)} %div.43, f32[1,5]{1,0:T(1,128)S(1)} %multiply_subtract_fusion.2, f32[]{:T(128)S(6)} %div.42, f32[1,1]{1,0:T(1,128)} %slice.361, f32[1,1]{1,0:T(1,128)} %constant.1.clone.1, ...), kind=kOutput, calls=%fused_computation.2 | convolution fusion | flops 15728675 | bytes 6291520 | tf_op jit(solution)/shard_map/si,iszxy->szxy/dot_general | solution.py:88
  229.7 3.5 collective-permute-start.12
  233.3 1.9 collective-permute-start.13
  236.3 2.5 collective-permute-done.13
  239.3 1.9 fusion.171
  243.1 3.8 collective-permute-start.14
  248.7 2.1 collective-permute-start.15
  250.8 3.1 pad_maximum_fusion.1
  258.3 10.0 %fusion.21 = f32[2,1,32,32,256]{4,3,2,1,0:T(8,128)S(1)} fusion(f32[2,1,32,32,256]{4,3,2,1,0:T(8,128)} %pad_maximum_fusion.1, f32[2,1,32,34,1]{4,3,2,1,0:T(8,128)} %copy.79, f32[2,1,32,1,256]{4,3,2,1,0:T(1,128)S(1)} %collective-permute-done.12, f32[2,1,32,1,256]{4,3,2,1,0:T(1,128)S(1)} %collective-permute-done.13, f32[1,1,32,32,256]{4,3,2,1,0:T(8,128)} %bitcast.208, ...), kind=kLoop, calls=%fused_computation.37 | loop fusion | flops 15204352 | bytes 12731392 | tf_op jit(solution)/shard_map/add | solution.py:56
  269.8 1.9 collective-permute-start.16
  271.7 2.4 collective-permute-start.17
  274.1 2.8 collective-permute-done.17
  279.8 4.8 %collective-permute-start.18 = (f32[1,32,34,1]{2,1,3,0:T(8,128)S(1)}, f32[1,32,34,1]{2,1,3,0:T(8,128)S(1)}, u32[]{:S(2)}, u32[]{:S(2)}) collective-permute-start(f32[1,32,34,1]{2,1,3,0:T(8,128)S(1)} %copy.80), channel_id=1, source_target_pairs={{1,0},{2,1},{3,2},{4,3},{5,4},{6,5},{7,6},{8,7},{9,8},{10,9},{11,1... | collective-permute-start | bytes 13064 | tf_op jit(solution)/shard_map/ppermute | solution.py:22
  286.0 1.9 collective-permute-start.19
  289.1 4.6 collective-permute-done.19
  294.9 10.1 %fusion.74 = f32[5,1,32,32,256]{4,3,2,1,0:T(8,128)} fusion(f32[5,1,32,32,256]{4,3,2,1,0:T(8,128)} %get-tuple-element.20, f32[1,32,32,256]{3,2,1,0:T(8,128)} %copy-done.7, f32[1,32,34,1]{3,2,1,0:T(8,128)} %copy.83, f32[1,32,1,256]{3,2,1,0:T(1,128)S(1)} %collective-permute-done.16, f32[1,32,1,256]{3,2,1,0:T(1,128)S(1)} %collective-permute-done.17, ...), kind=kLoop, calls=%fused_computation.135 | loop fusion | flops 6553600 | bytes 9572352
  308.1 28.2 %fusion.49 = f32[5,5]{1,0:T(8,128)S(1)} fusion(f32[5,32,32,256]{3,2,1,0:T(8,128)} %bitcast.46), kind=kOutput, calls=%fused_computation.97 | convolution fusion | flops 78643200 | bytes 5242980 | tf_op jit(solution)/shard_map/iszxy,jszxy->sij/dot_general | solution.py:114
  336.3 14.5 %fusion.4 = f32[1,32,32,256]{3,0,2,1:T(1,128)} fusion(f32[5,32,32,256]{3,2,1,0:T(8,128)} %bitcast.11, f32[1,5]{1,0:T(1,128)S(1)} %multiply_add_fusion.1, f32[]{:T(128)S(6)} %div.42, f32[]{:T(128)S(6)} %div.40, f32[5,5]{1,0:T(8,128)S(1)} %fusion.137), kind=kOutput, calls=%fused_computation.4 | convolution fusion | flops 15728655 | bytes 6292488 | tf_op jit(solution)/shard_map/si,iszxy->szxy/dot_general | solution.py:88
  350.8 60.7 %psum.15 = f32[5,5]{1,0:T(8,128)S(1)} all-reduce(f32[5,5]{1,0:T(8,128)S(1)} %fusion.49), channel_id=1, replica_groups=mesh['gx'=8,'gy'=16] {'gx','gy'}, use_global_device_ids=true, to_apply=%region_1.2 | all-reduce | flops 25 | bytes 200 | tf_op jit(solution)/shard_map/psum | solution.py:115
  420.3 13.6 %fusion.6 = f32[1,32,32,256]{3,0,2,1:T(1,128)S(1)} fusion(f32[5,32,32,256]{3,2,1,0:T(8,128)} %bitcast.46, f32[1,5]{1,0:T(1,128)S(1)} %multiply_add_fusion, f32[]{:T(128)S(6)} %div.46, f32[]{:T(128)S(6)} %div.44, f32[5,5]{1,0:T(8,128)S(1)} %fusion.137), kind=kOutput, calls=%fused_computation.6 | convolution fusion | flops 15728655 | bytes 6292488 | tf_op jit(solution)/shard_map/si,iszxy->szxy/dot_general | solution.py:88
  434.2 3.2 collective-permute-start.20
  437.4 1.9 collective-permute-start.21
  439.3 3.3 collective-permute-done.21
  445.5 4.3 collective-permute-start.22
  451.2 1.9 collective-permute-start.23
  454.3 4.6 collective-permute-done.23
  460.1 10.7 %fusion.81 = (f32[1,32,32,256]{3,2,1,0:T(8,128)}, f32[1,32,32,256]{3,2,1,0:T(8,128)}, f32[1,32,32,256]{3,2,1,0:T(8,128)}) fusion(f32[1,32,32,256]{3,2,1,0:T(8,128)S(1)} %copy-done.1, f32[1,32,32,256]{3,2,1,0:T(8,128)} %copy-done.5, f32[1,32,34,1]{3,2,1,0:T(8,128)} %copy.89, f32[1,32,1,256]{3,2,1,0:T(1,128)S(1)} %collective-permute-done.20, ...), kind=kLoop, calls=%fused_computation.142 | loop fusion | flops 6815744 | bytes 10672064 | tf_op jit(solution)/shard_map/sub | solution.py:121
  (145 shorter events, 77.5 us)
Async XLA Ops:
  0.6 12.5 %copy-start.1 = (f32[1,32,32,256]{3,2,1,0:T(8,128)S(1)}, f32[1,32,32,256]{3,2,1,0:T(8,128)}, u32[]{:S(2)}) copy-start(f32[1,32,32,256]{3,2,1,0:T(8,128)} %param.3) | copy-start | bytes 3145732
  0.6 13.6 %copy-start.23 = (f32[1,32,32,256]{3,2,1,0:T(8,128)S(1)}, f32[1,32,32,256]{3,2,1,0:T(8,128)}, u32[]{:S(2)}) copy-start(f32[1,32,32,256]{3,2,1,0:T(8,128)} %param.2) | copy-start | bytes 3145732
  1.9 12.3 %collective-permute-start = (f32[1,32,2,256]{3,2,1,0:T(2,128)S(1)}, f32[1,32,2,256]{3,2,1,0:T(2,128)S(1)}, u32[]{:S(2)}, u32[]{:S(2)}) collective-permute-start(f32[1,32,2,256]{3,2,1,0:T(2,128)S(1)} %get-tuple-element.45), channel_id=1, source_target_pairs={{0,16},{16,32},{32,48},{48,64},{64,80},{80,96},{96,112},{1,17},{17... | collective-permute-start | bytes 196616 | tf_op jit(solution)/shard_map/ppermute | solution.py:20
  3.8 10.4 %collective-permute-start.1 = (f32[1,32,2,256]{3,2,1,0:T(2,128)S(1)}, f32[1,32,2,256]{3,2,1,0:T(2,128)S(1)}, u32[]{:S(2)}, u32[]{:S(2)}) collective-permute-start(f32[1,32,2,256]{3,2,1,0:T(2,128)S(1)} %get-tuple-element.46), channel_id=1, source_target_pairs={{16,0},{32,16},{48,32},{64,48},{80,64},{96,80},{112,96},{17,1},{33... | collective-permute-start | bytes 196616 | tf_op jit(solution)/shard_map/ppermute | solution.py:22
  8.8 16.4 %collective-permute-start.4 = (f32[2,1,32,1,256]{4,3,2,1,0:T(1,128)S(1)}, f32[2,1,32,1,256]{4,3,2,1,0:T(1,128)S(1)}, u32[]{:S(2)}, u32[]{:S(2)}) collective-permute-start(f32[2,1,32,1,256]{4,3,2,1,0:T(1,128)S(1)} %get-tuple-element.48), channel_id=1, source_target_pairs={{16,0},{32,16},{48,32},{64,48},{80,64},{96,80},{112,96},{17,1},{33... | collective-permute-start | bytes 196616 | tf_op jit(solution)/shard_map/ppermute | solution.py:22
  10.7 14.5 %collective-permute-start.5 = (f32[2,1,32,1,256]{4,3,2,1,0:T(1,128)S(1)}, f32[2,1,32,1,256]{4,3,2,1,0:T(1,128)S(1)}, u32[]{:S(2)}, u32[]{:S(2)}) collective-permute-start(f32[2,1,32,1,256]{4,3,2,1,0:T(1,128)S(1)} %get-tuple-element.47), channel_id=1, source_target_pairs={{0,16},{16,32},{32,48},{48,64},{64,80},{80,96},{96,112},{1,17},{17... | collective-permute-start | bytes 196616 | tf_op jit(solution)/shard_map/ppermute | solution.py:20
  16.9 25.9 %collective-permute-start.2 = (f32[1,32,36,2]{2,1,3,0:T(8,128)S(1)}, f32[1,32,36,2]{2,1,3,0:T(8,128)S(1)}, u32[]{:S(2)}, u32[]{:S(2)}) collective-permute-start(f32[1,32,36,2]{2,1,3,0:T(8,128)S(1)} %copy.62), channel_id=1, source_target_pairs={{0,1},{1,2},{2,3},{3,4},{4,5},{5,6},{6,7},{7,8},{8,9},{9,10},{10,1... | collective-permute-start | bytes 27656 | tf_op jit(solution)/shard_map/ppermute | solution.py:20
  21.0 22.1 %collective-permute-start.3 = (f32[1,32,36,2]{2,1,3,0:T(8,128)S(1)}, f32[1,32,36,2]{2,1,3,0:T(8,128)S(1)}, u32[]{:S(2)}, u32[]{:S(2)}) collective-permute-start(f32[1,32,36,2]{2,1,3,0:T(8,128)S(1)} %copy.63), channel_id=1, source_target_pairs={{1,0},{2,1},{3,2},{4,3},{5,4},{6,5},{7,6},{8,7},{9,8},{10,9},{11,1... | collective-permute-start | bytes 27656 | tf_op jit(solution)/shard_map/ppermute | solution.py:22
  28.8 8.0 %collective-permute-start.6 = (f32[2,1,32,34,1]{3,2,4,1,0:T(8,128)S(1)}, f32[2,1,32,34,1]{3,2,4,1,0:T(8,128)S(1)}, u32[]{:S(2)}, u32[]{:S(2)}) collective-permute-start(f32[2,1,32,34,1]{3,2,4,1,0:T(8,128)S(1)} %copy.66), channel_id=1, source_target_pairs={{1,0},{2,1},{3,2},{4,3},{5,4},{6,5},{7,6},{8,7},{9,8},{10,9},{11,1... | collective-permute-start | bytes 26120 | tf_op jit(solution)/shard_map/ppermute | solution.py:22
  33.1 7.9 %collective-permute-start.7 = (f32[2,1,32,34,1]{3,2,4,1,0:T(8,128)S(1)}, f32[2,1,32,34,1]{3,2,4,1,0:T(8,128)S(1)}, u32[]{:S(2)}, u32[]{:S(2)}) collective-permute-start(f32[2,1,32,34,1]{3,2,4,1,0:T(8,128)S(1)} %copy.68), channel_id=1, source_target_pairs={{0,1},{1,2},{2,3},{3,4},{4,5},{5,6},{6,7},{7,8},{8,9},{9,10},{10,1... | collective-permute-start | bytes 26120 | tf_op jit(solution)/shard_map/ppermute | solution.py:20
  36.8 7.5 %copy-start.24 = (f32[1,32,32,256]{3,2,1,0:T(8,128)S(1)}, f32[1,32,32,256]{3,2,1,0:T(8,128)}, u32[]{:S(2)}) copy-start(f32[1,32,32,256]{3,2,1,0:T(8,128)} %param.2) | copy-start | bytes 3145732
  47.5 2.4 copy-start
  47.8 1.5 copy-start.2
  49.9 1.4 copy-start.10
  49.9 2.6 copy-start.18
  49.9 3.8 copy-start.21
  49.9 4.5 copy-start.22
  51.2 6.5 %copy-start.12 = (f32[32,32,256]{2,1,0:T(8,128)}, f32[32,32,256]{2,1,0:T(8,128)S(1)}, u32[]{:S(2)}) copy-start(f32[32,32,256]{2,1,0:T(8,128)S(1)} %get-tuple-element.27) | copy-start | bytes 3145732
  51.2 6.5 %copy-start.13 = (f32[32,32,256]{2,1,0:T(8,128)}, f32[32,32,256]{2,1,0:T(8,128)S(1)}, u32[]{:S(2)}) copy-start(f32[32,32,256]{2,1,0:T(8,128)S(1)} %get-tuple-element.28) | copy-start | bytes 3145732
  51.2 6.5 %copy-start.14 = (f32[32,32,256]{2,1,0:T(8,128)}, f32[32,32,256]{2,1,0:T(8,128)S(1)}, u32[]{:S(2)}) copy-start(f32[32,32,256]{2,1,0:T(8,128)S(1)} %get-tuple-element.49) | copy-start | bytes 3145732
  51.2 6.5 %copy-start.15 = (f32[32,32,256]{2,1,0:T(8,128)}, f32[32,32,256]{2,1,0:T(8,128)S(1)}, u32[]{:S(2)}) copy-start(f32[32,32,256]{2,1,0:T(8,128)S(1)} %get-tuple-element.50) | copy-start | bytes 3145732
  57.7 8.8 %copy-start.16 = (f32[2,1,32,32,256]{4,3,2,1,0:T(8,128)}, f32[2,1,32,32,256]{4,3,2,1,0:T(8,128)S(1)}, u32[]{:S(2)}) copy-start(f32[2,1,32,32,256]{4,3,2,1,0:T(8,128)S(1)} %fusion.15) | copy-start | bytes 6291460
  59.2 8.7 %copy-start.6 = (f32[1,32,32,256]{3,2,1,0:T(8,128)}, f32[1,32,32,256]{3,2,1,0:T(8,128)S(1)}, u32[]{:S(2)}) copy-start(f32[1,32,32,256]{3,2,1,0:T(8,128)S(1)} %get-tuple-element.23) | copy-start | bytes 3145732
  59.2 4.4 collective-permute-start.8
  61.1 5.2 %collective-permute-start.9 = (f32[1,32,1,256]{3,2,1,0:T(1,128)S(1)}, f32[1,32,1,256]{3,2,1,0:T(1,128)S(1)}, u32[]{:S(2)}, u32[]{:S(2)}) collective-permute-start(f32[1,32,1,256]{3,2,1,0:T(1,128)S(1)} %get-tuple-element.43), channel_id=1, source_target_pairs={{0,16},{16,32},{32,48},{48,64},{64,80},{80,96},{96,112},{1,17},{17... | collective-permute-start | bytes 98312 | tf_op jit(solution)/shard_map/ppermute | solution.py:20
  69.2 7.8 %collective-permute-start.10 = (f32[1,32,34,1]{2,1,3,0:T(8,128)S(1)}, f32[1,32,34,1]{2,1,3,0:T(8,128)S(1)}, u32[]{:S(2)}, u32[]{:S(2)}) collective-permute-start(f32[1,32,34,1]{2,1,3,0:T(8,128)S(1)} %copy.70), channel_id=1, source_target_pairs={{1,0},{2,1},{3,2},{4,3},{5,4},{6,5},{7,6},{8,7},{9,8},{10,9},{11,1... | collective-permute-start | bytes 13064 | tf_op jit(solution)/shard_map/ppermute | solution.py:22
  74.0 7.7 %collective-permute-start.11 = (f32[1,32,34,1]{2,1,3,0:T(8,128)S(1)}, f32[1,32,34,1]{2,1,3,0:T(8,128)S(1)}, u32[]{:S(2)}, u32[]{:S(2)}) collective-permute-start(f32[1,32,34,1]{2,1,3,0:T(8,128)S(1)} %copy.72), channel_id=1, source_target_pairs={{0,1},{1,2},{2,3},{3,4},{4,5},{5,6},{6,7},{7,8},{8,9},{9,10},{10,1... | collective-permute-start | bytes 13064 | tf_op jit(solution)/shard_map/ppermute | solution.py:20
  93.6 2.0 copy-start.17
  229.5 9.3 %copy-start.3 = (f32[1,32,32,256]{3,2,1,0:T(8,128)}, f32[1,32,32,256]{3,2,1,0:T(8,128)S(1)}, u32[]{:S(2)}) copy-start(f32[1,32,32,256]{3,2,1,0:T(8,128)S(1)} %copy.145) | copy-start | bytes 3145732
  229.6 9.2 %copy-start.4 = (f32[1,32,32,256]{3,2,1,0:T(8,128)}, f32[1,32,32,256]{3,2,1,0:T(8,128)S(1)}, u32[]{:S(2)}) copy-start(f32[1,32,32,256]{3,2,1,0:T(8,128)S(1)} %copy.144) | copy-start | bytes 3145732
  229.7 6.6 %collective-permute-start.12 = (f32[2,1,32,1,256]{4,3,2,1,0:T(1,128)S(1)}, f32[2,1,32,1,256]{4,3,2,1,0:T(1,128)S(1)}, u32[]{:S(2)}, u32[]{:S(2)}) collective-permute-start(f32[2,1,32,1,256]{4,3,2,1,0:T(1,128)S(1)} %get-tuple-element.22), channel_id=1, source_target_pairs={{16,0},{32,16},{48,32},{64,48},{80,64},{96,80},{112,96},{17,1},{33... | collective-permute-start | bytes 196616 | tf_op jit(solution)/shard_map/ppermute | solution.py:22
  233.3 5.6 %collective-permute-start.13 = (f32[2,1,32,1,256]{4,3,2,1,0:T(1,128)S(1)}, f32[2,1,32,1,256]{4,3,2,1,0:T(1,128)S(1)}, u32[]{:S(2)}, u32[]{:S(2)}) collective-permute-start(f32[2,1,32,1,256]{4,3,2,1,0:T(1,128)S(1)} %get-tuple-element.21), channel_id=1, source_target_pairs={{0,16},{16,32},{32,48},{48,64},{64,80},{80,96},{96,112},{1,17},{17... | collective-permute-start | bytes 196616 | tf_op jit(solution)/shard_map/ppermute | solution.py:20
  243.1 10.9 %collective-permute-start.14 = (f32[2,1,32,34,1]{3,2,4,1,0:T(8,128)S(1)}, f32[2,1,32,34,1]{3,2,4,1,0:T(8,128)S(1)}, u32[]{:S(2)}, u32[]{:S(2)}) collective-permute-start(f32[2,1,32,34,1]{3,2,4,1,0:T(8,128)S(1)} %copy.76), channel_id=1, source_target_pairs={{1,0},{2,1},{3,2},{4,3},{5,4},{6,5},{7,6},{8,7},{9,8},{10,9},{11,1... | collective-permute-start | bytes 26120 | tf_op jit(solution)/shard_map/ppermute | solution.py:22
  248.7 7.9 %collective-permute-start.15 = (f32[2,1,32,34,1]{3,2,4,1,0:T(8,128)S(1)}, f32[2,1,32,34,1]{3,2,4,1,0:T(8,128)S(1)}, u32[]{:S(2)}, u32[]{:S(2)}) collective-permute-start(f32[2,1,32,34,1]{3,2,4,1,0:T(8,128)S(1)} %copy.78), channel_id=1, source_target_pairs={{0,1},{1,2},{2,3},{3,4},{4,5},{5,6},{6,7},{7,8},{8,9},{9,10},{10,1... | collective-permute-start | bytes 26120 | tf_op jit(solution)/shard_map/ppermute | solution.py:20
  268.3 8.8 %copy-start.19 = (f32[2,1,32,32,256]{4,3,2,1,0:T(8,128)}, f32[2,1,32,32,256]{4,3,2,1,0:T(8,128)S(1)}, u32[]{:S(2)}) copy-start(f32[2,1,32,32,256]{4,3,2,1,0:T(8,128)S(1)} %fusion.21) | copy-start | bytes 6291460
  269.7 8.7 %copy-start.7 = (f32[1,32,32,256]{3,2,1,0:T(8,128)}, f32[1,32,32,256]{3,2,1,0:T(8,128)S(1)}, u32[]{:S(2)}) copy-start(f32[1,32,32,256]{3,2,1,0:T(8,128)S(1)} %get-tuple-element.19) | copy-start | bytes 3145732
  269.8 4.3 collective-permute-start.16
  271.7 5.2 %collective-permute-start.17 = (f32[1,32,1,256]{3,2,1,0:T(1,128)S(1)}, f32[1,32,1,256]{3,2,1,0:T(1,128)S(1)}, u32[]{:S(2)}, u32[]{:S(2)}) collective-permute-start(f32[1,32,1,256]{3,2,1,0:T(1,128)S(1)} %get-tuple-element.41), channel_id=1, source_target_pairs={{0,16},{16,32},{32,48},{48,64},{64,80},{80,96},{96,112},{1,17},{17... | collective-permute-start | bytes 98312 | tf_op jit(solution)/shard_map/ppermute | solution.py:20
  279.8 8.2 %collective-permute-start.18 = (f32[1,32,34,1]{2,1,3,0:T(8,128)S(1)}, f32[1,32,34,1]{2,1,3,0:T(8,128)S(1)}, u32[]{:S(2)}, u32[]{:S(2)}) collective-permute-start(f32[1,32,34,1]{2,1,3,0:T(8,128)S(1)} %copy.80), channel_id=1, source_target_pairs={{1,0},{2,1},{3,2},{4,3},{5,4},{6,5},{7,6},{8,7},{9,8},{10,9},{11,1... | collective-permute-start | bytes 13064 | tf_op jit(solution)/shard_map/ppermute | solution.py:22
  286.0 7.7 %collective-permute-start.19 = (f32[1,32,34,1]{2,1,3,0:T(8,128)S(1)}, f32[1,32,34,1]{2,1,3,0:T(8,128)S(1)}, u32[]{:S(2)}, u32[]{:S(2)}) collective-permute-start(f32[1,32,34,1]{2,1,3,0:T(8,128)S(1)} %copy.82), channel_id=1, source_target_pairs={{0,1},{1,2},{2,3},{3,4},{4,5},{5,6},{6,7},{7,8},{8,9},{9,10},{10,1... | collective-permute-start | bytes 13064 | tf_op jit(solution)/shard_map/ppermute | solution.py:20
  294.9 10.1 %copy-start.9 = (f32[1,32,32,256]{3,0,2,1:T(1,128)S(1)}, f32[1,32,32,256]{3,0,2,1:T(1,128)}, u32[]{:S(2)}) copy-start(f32[1,32,32,256]{3,0,2,1:T(1,128)} %fusion) | copy-start | bytes 3145732
  305.0 2.0 copy-start.20
  420.3 13.7 %copy-start.25 = (f32[1,32,32,256]{3,0,2,1:T(1,128)S(1)}, f32[1,32,32,256]{3,0,2,1:T(1,128)}, u32[]{:S(2)}) copy-start(f32[1,32,32,256]{3,0,2,1:T(1,128)} %fusion.4) | copy-start | bytes 3145732
  434.1 9.9 %copy-start.5 = (f32[1,32,32,256]{3,2,1,0:T(8,128)}, f32[1,32,32,256]{3,2,1,0:T(8,128)S(1)}, u32[]{:S(2)}) copy-start(f32[1,32,32,256]{3,2,1,0:T(8,128)S(1)} %fusion.117) | copy-start | bytes 3145732
  434.2 5.1 %collective-permute-start.20 = (f32[1,32,1,256]{3,2,1,0:T(1,128)S(1)}, f32[1,32,1,256]{3,2,1,0:T(1,128)S(1)}, u32[]{:S(2)}, u32[]{:S(2)}) collective-permute-start(f32[1,32,1,256]{3,2,1,0:T(1,128)S(1)} %get-tuple-element.40), channel_id=1, source_target_pairs={{16,0},{32,16},{48,32},{64,48},{80,64},{96,80},{112,96},{17,1},{33... | collective-permute-start | bytes 98312 | tf_op jit(solution)/shard_map/ppermute | solution.py:22
  437.4 5.2 %collective-permute-start.21 = (f32[1,32,1,256]{3,2,1,0:T(1,128)S(1)}, f32[1,32,1,256]{3,2,1,0:T(1,128)S(1)}, u32[]{:S(2)}, u32[]{:S(2)}) collective-permute-start(f32[1,32,1,256]{3,2,1,0:T(1,128)S(1)} %get-tuple-element.39), channel_id=1, source_target_pairs={{0,16},{16,32},{32,48},{48,64},{64,80},{80,96},{96,112},{1,17},{17... | collective-permute-start | bytes 98312 | tf_op jit(solution)/shard_map/ppermute | solution.py:20
  445.5 7.7 %collective-permute-start.22 = (f32[1,32,34,1]{2,1,3,0:T(8,128)S(1)}, f32[1,32,34,1]{2,1,3,0:T(8,128)S(1)}, u32[]{:S(2)}, u32[]{:S(2)}) collective-permute-start(f32[1,32,34,1]{2,1,3,0:T(8,128)S(1)} %copy.86), channel_id=1, source_target_pairs={{1,0},{2,1},{3,2},{4,3},{5,4},{6,5},{7,6},{8,7},{9,8},{10,9},{11,1... | collective-permute-start | bytes 13064 | tf_op jit(solution)/shard_map/ppermute | solution.py:22
  451.2 7.7 %collective-permute-start.23 = (f32[1,32,34,1]{2,1,3,0:T(8,128)S(1)}, f32[1,32,34,1]{2,1,3,0:T(8,128)S(1)}, u32[]{:S(2)}, u32[]{:S(2)}) collective-permute-start(f32[1,32,34,1]{2,1,3,0:T(8,128)S(1)} %copy.88), channel_id=1, source_target_pairs={{0,1},{1,2},{2,3},{3,4},{4,5},{5,6},{6,7},{7,8},{8,9},{9,10},{10,1... | collective-permute-start | bytes 13064 | tf_op jit(solution)/shard_map/ppermute | solution.py:20
  (2 other events, 2.6 us)
where the time goes:
time: 480 us; the launch traced here: 471 us
  blocking collectives  123 us (26%)
  matrix products  122 us (25%)
  starting transfers between devices  67.5 us (14%)
  local copies, waits for them, and re-layouts  62 us (13%)
  other arithmetic  57.7 us (12%)
  waiting for transfers between devices  27.9 us (6%)
  between operations  11.1 us (2%)
    psum x2, blocking collectives, on_device(): gram_matrix = lax.psum(local_gram, ('gx', 'gy'))  123 us
    dot_general x4, matrix products, combine(): return jnp.einsum('si,iszxy->szxy', coef_in, basis, precision=exact_mode)  57.4 us
    dot_general x2, matrix products, on_device(): jnp.einsum('iszxy,jszxy->sij', basis, basis, precision=exact_mode)  56.2 us
    ppermute x12, starting transfers between devices, padded(): lax.ppermute(head, axis, [((i + 1) % count, i) for i in range(ends)])  40.3 us
    ppermute x12, waiting for transfers between devices, padded(): lax.ppermute(tail, axis, [(i, (i + 1) % count) for i in range(ends)])  27.8 us
    ppermute x12, starting transfers between devices, padded(): lax.ppermute(tail, axis, [(i, (i + 1) % count) for i in range(ends)])  27.2 us
    unnamed x2, other arithmetic  20.7 us
    slice x11, local copies, waits for them, and re-layouts, padded(): head = lax.slice_in_dim(cells, 0, width, axis=dim)  15.4 us
  transfers between devices with their start and end apart: 24, of which 9 were waited for; matrix products, arithmetic and copies ran while one was open for 7% of the time, Pallas kernels for 0%

commit v1 on v0

v1 whole, which is shorter than its diff:
```python
import functools

import jax
import jax.numpy as jnp
from jax import lax
from jax.experimental import pallas as pl
from jax.experimental.pallas import tpu as pltpu
from jax.sharding import PartitionSpec as P

MESH = pl.DeviceIdType.MESH
F32 = jnp.float32
TOP = 8
ROWS = 48
WIDE = (4, 12, 20, 28, 36)
OWN = (8, 16, 24, 32)
DIRS = ((0, 1), (0, -1), (1, 0), (-1, 0), (1, 1), (1, -1), (-1, 1), (-1, -1))


def iota(dim):
    return lax.broadcasted_iota(jnp.int32, (8, 128), dim)


def roll(value, amount):
    return pltpu.roll(value, amount % 128 if isinstance(amount, int) else amount, 1)


def two_sum(a, b):
    s = a + b
    t = s - a
    return s, (a - (s - t)) + (b - t)


def quick(a, b):
    s = a + b
    return s, b - (s - a)


def pair_add(x, y):
    s, e = two_sum(x[0], y[0])
    return quick(s, e + (x[1] + y[1]))


def halves(a):
    t = a * 4097.0
    hi = t - (t - a)
    return hi, a - hi


def pair_mul(x, y):
    p = x[0] * y[0]
    xh, xl = halves(x[0])
    yh, yl = halves(y[0])
    e = ((xh * yh - p) + xh * yl + xl * yh) + xl * yl
    return quick(p, e + (x[0] * y[1] + x[1] * y[0]))


def neg(x):
    return (-x[0], -x[1])


def pair_div(x, y):
    q = x[0] / y[0]
    zero = jnp.zeros_like(q)
    rest = pair_add(x, neg(pair_mul(y, (q, zero))))
    return quick(q, rest[0] / y[0])


def coefficients(moments):
    resid, direc = dict(enumerate(moments)), dict(enumerate(moments))
    steps, ratios = [], []
    for k in range(4):
        step = pair_div(resid[k], direc[k + 1])
        steps.append(step)
        if k == 3:
            break
        fresh = {}
        for l in range(k + 1, 7 - k):
            fresh[l] = pair_add(resid[l], neg(pair_mul(step, direc[l + 1])))
        ratio = neg(pair_div(pair_mul(step, fresh[k + 1]), resid[k]))
        ratios.append(ratio)
        direc = {l: pair_add(fresh[l], pair_mul(ratio, direc[l])) for l in fresh}
        resid = fresh
    a = [s[0] for s in steps]
    b = [r[0] for r in ratios]
    one = jnp.ones_like(a[0])
    r, p = [one], [one]
    x = [a[0]]
    for k in range(3):
        moved = [None] + [a[k] * c for c in p]
        r = [
            moved[m] * -1.0 if m >= len(r) else (r[m] if moved[m] is None else r[m] - moved[m])
            for m in range(len(moved))
        ]
        p = [r[m] + b[k] * p[m] if m < len(p) else r[m] for m in range(len(r))]
        x = [x[m] + a[k + 1] * p[m] if m < len(x) else a[k + 1] * p[m] for m in range(len(p))]
    return x


def tree(hi, lo):
    for shift in (4, 2, 1):
        hi, lo = pair_add((hi, lo), (pltpu.roll(hi, shift, 0), pltpu.roll(lo, shift, 0)))
    return hi, lo


def build(nz, gx, gy, lp_ref, src_ref, v0, v1, v2, v3, v4, tx, ty, q, coef,
          lp, w, tz, s_own, s_left, s_right, ws, txs, tys, tzs, b0, b1, b2, b3, fzs,
          send_row, red_a, red_b, load_sem, x_send, x_recv, s_send, s_recv, a_send, a_recv, c_send, c_recv):
    i = lax.axis_index("gx")
    j = lax.axis_index("gy")
    zp_count = nz // 8
    fields = (v0, v1, v2, v3, v4)
    strips = (b0, b1, b2, b3)
    lane, sub = iota(1), iota(0)
    l16 = lane % 16

    barrier = pltpu.get_barrier_semaphore()
    for d in range(1, gx):
        pl.semaphore_signal(barrier, inc=1, device_id=(lax.rem(i + d, gx), j), device_id_type=MESH)
    for d in range(1, gy):
        pl.semaphore_signal(barrier, inc=1, device_id=(i, lax.rem(j + d, gy)), device_id_type=MESH)

    def inside(di, dj):
        ok = None
        for cond in (
            [] if di == 0 else [i < gx - 1] if di > 0 else [i > 0]
        ) + ([] if dj == 0 else [j < gy - 1] if dj > 0 else [j > 0]):
            ok = cond if ok is None else jnp.logical_and(ok, cond)
        return ok

    for di, dj in DIRS[4:]:
        @pl.when(inside(di, dj))
        def _():
            pl.semaphore_signal(barrier, inc=1, device_id=(i + di, j + dj), device_id_type=MESH)

    loads = []
    for n, (source, target) in enumerate(((src_ref, v0), (lp_ref, lp))):
        for h in range(2):
            copy = pltpu.make_async_copy(
                source.at[0, :, :, pl.ds(128 * h, 128)],
                target.at[h, :, pl.ds(TOP, 32), :],
                load_sem.at[2 * n + h],
            )
            copy.start()
            loads.append(copy)

    zero4 = jnp.zeros((4, 128), F32)

    @pl.when(i == 0)
    def _():
        def fill(z, carry):
            for h in range(2):
                v0[h, z, 4:8] = zero4
                lp[h, z, 4:8] = zero4
            return carry
        lax.fori_loop(0, nz, fill, 0)
        for zp in range(zp_count):
            for buf in (s_own, s_left, s_right):
                buf[zp, 4:8] = zero4

    @pl.when(i == gx - 1)
    def _():
        def fill(z, carry):
            for h in range(2):
                v0[h, z, 40:44] = zero4
                lp[h, z, 40:44] = zero4
            return carry
        lax.fori_loop(0, nz, fill, 0)
        for zp in range(zp_count):
            for buf in (s_own, s_left, s_right):
                buf[zp, 40:44] = zero4

    for edge, buf in ((j == 0, s_left), (j == gy - 1, s_right)):
        @pl.when(edge)
        def _():
            for zp in range(zp_count):
                buf[zp, 4:8] = zero4
                buf[zp, 40:44] = zero4
                for r in OWN:
                    buf[zp, r:r + 8] = jnp.zeros((8, 128), F32)

    for n, red in ((gx, red_a), (gy, red_b)):
        for r in range(n, red.shape[0]):
            red[r:r + 1, :] = jnp.zeros((1, 128), F32)

    inner_i = (i > 0).astype(jnp.int32) + (i < gx - 1).astype(jnp.int32)
    inner_j = (j > 0).astype(jnp.int32) + (j < gy - 1).astype(jnp.int32)
    pl.semaphore_wait(barrier, gx - 1 + gy - 1 + inner_i * inner_j)

    x_copies = []
    for step, first, land in ((1, 28, 4), (-1, 0, 40)):
        group = []
        for n, (source, target) in enumerate(((lp_ref, lp), (src_ref, v0))):
            for h in range(2):
                slot = (0 if step > 0 else 4) + 2 * n + h
                group.append(pltpu.make_async_remote_copy(
                    src_ref=source.at[0, :, pl.ds(first, 4), pl.ds(128 * h, 128)],
                    dst_ref=target.at[h, :, pl.ds(land, 4), :],
                    send_sem=x_send.at[slot],
                    recv_sem=x_recv.at[slot],
                    device_id=(i + step, j),
                    device_id_type=MESH,
                ))
        x_copies.append((step, group))

        @pl.when(inside(step, 0))
        def _():
            for copy in group:
                copy.start()

    for copy in loads:
        copy.wait()

    def pack(zp, carry):
        for r in OWN:
            packed = jnp.zeros((8, 128), F32)
            for g in range(8):
                z = g * zp_count + zp
                fld = jnp.where(lane < 64, v0[0, z, r:r + 8], v0[1, z, r:r + 8])
                log = jnp.where(lane < 64, lp[0, z, r:r + 8], lp[1, z, r:r + 8])
                both = jnp.where(l16 < 8, roll(log, 16 * g + 4), roll(fld, 16 * g + 12))
                packed = jnp.where(lane // 16 == g, both, packed)
            s_own[zp, r:r + 8] = packed
        return carry

    lax.fori_loop(0, zp_count, pack, 0)

    s_copies = []
    for n, (di, dj) in enumerate(DIRS):
        target = s_own if dj == 0 else s_left if dj > 0 else s_right
        if di == 0:
            first, land, count = 8, 8, 32
        elif di > 0:
            first, land, count = 36, 4, 4
        else:
            first, land, count = 8, 40, 4
        copy = pltpu.make_async_remote_copy(
            src_ref=s_own.at[:, pl.ds(first, count), :],
            dst_ref=target.at[:, pl.ds(land, count), :],
            send_sem=s_send.at[n],
            recv_sem=s_recv.at[n],
            device_id=(i + di, j + dj),
            device_id_type=MESH,
        )
        s_copies.append((di, dj, copy))

    for di, dj, copy in s_copies[4:] + s_copies[:4]:
        @pl.when(inside(di, dj))
        def _():
            copy.start()

    def invert(z, carry):
        for h in range(2):
            for r in OWN:
                w[h, z, r:r + 8] = jnp.exp(-lp[h, z, r:r + 8])
        return carry

    lax.fori_loop(0, nz, invert, 0)

    def faces(z, carry):
        above = jnp.minimum(z + 1, nz - 1)
        top = jnp.where(z < nz - 1, 2.0, 0.0)
        for r in OWN:
            w0, w1 = w[0, z, r:r + 8], w[1, z, r:r + 8]
            n0, n1 = roll(w0, -1), roll(w1, -1)
            ty[0, z, r:r + 8] = 2.0 / (w0 + jnp.where(lane == 127, n1, n0))
            ty[1, z, r:r + 8] = 2.0 / (w1 + n1)
            for h, mid in ((0, w0), (1, w1)):
                tx[h, z, r:r + 8] = 2.0 / (mid + w[h, z, r + 1:r + 9])
                tz[h, z, r:r + 8] = top / (mid + w[h, above, r:r + 8])
        return carry

    lax.fori_loop(0, nz, faces, 0)

    for di, dj, copy in s_copies:
        @pl.when(inside(-di, -dj))
        def _():
            copy.wait_recv()

    for zp in range(zp_count):
        for r in WIDE:
            own, left, right = (s[zp, r:r + 8] for s in (s_own, s_left, s_right))
            moved = roll(jnp.where(l16 < 12, left, own), -8)
            b0[zp, r:r + 8] = jnp.where(l16 < 8, moved, jnp.where(l16 < 12, own, right))
            moved = roll(jnp.where(l16 < 4, own, right), 8)
            log = jnp.where(l16 < 8, jnp.where(l16 < 4, left, own), moved)
            ws[zp, r:r + 8] = jnp.exp(-log)
    for zp in range(zp_count):
        for r in WIDE:
            mid = ws[zp, r:r + 8]
            txs[zp, r:r + 8] = 2.0 / (mid + ws[zp, r + 1:r + 9])
            tys[zp, r:r + 8] = 2.0 / (mid + roll(mid, -1))
            if zp < zp_count - 1:
                tzs[zp, r:r + 8] = 2.0 / (mid + ws[zp + 1, r:r + 8])
            else:
                tzs[zp, r:r + 8] = jnp.where(lane < 112, 2.0 / (mid + roll(ws[0, r:r + 8], -16)), 0.0)
    keep_cols = jnp.logical_and(jnp.logical_or(l16 >= 4, j > 0), jnp.logical_or(l16 < 12, j < gy - 1))
    keep_top = jnp.logical_or(sub >= 4, i > 0)
    keep_bottom = jnp.logical_or(sub < 4, i < gx - 1)
    for k in range(4):
        field = strips[k]
        if k < 3:
            for zp in range(zp_count):
                for r in WIDE:
                    mid = field[zp, r:r + 8]
                    above = field[zp + 1, r:r + 8] if zp < zp_count - 1 else roll(field[0, r:r + 8], -16)
                    fzs[zp, r:r + 8] = tzs[zp, r:r + 8] * (mid - above)
        for zp in range(zp_count):
            for r in WIDE:
                mid = field[zp, r:r + 8]
                fy = tys[zp, r:r + 8] * (mid - roll(mid, -1))
                q[k, zp, r:r + 8] = jnp.where(l16 == 8, roll(fy, 5), roll(fy, -4))
                if k == 3:
                    continue
                below = fzs[zp - 1, r:r + 8] if zp else roll(fzs[zp_count - 1, r:r + 8], 16)
                total = txs[zp, r:r + 8] * (mid - field[zp, r + 1:r + 9])
                total = total + txs[zp, r - 1:r + 7] * (mid - field[zp, r - 1:r + 7])
                total = total + (fy - roll(fy, 1)) + (fzs[zp, r:r + 8] - below)
                keep = keep_cols
                if r == 4:
                    keep = jnp.logical_and(keep, keep_top)
                if r == 36:
                    keep = jnp.logical_and(keep, keep_bottom)
                strips[k + 1][zp, r:r + 8] = jnp.where(keep, total, 0.0)

    for step, group in x_copies:
        @pl.when(inside(-step, 0))
        def _():
            for copy in group:
                copy.wait_recv()

    def invert_rim(z, carry):
        for h in range(2):
            both = jnp.exp(-jnp.where(sub < 4, lp[h, z, 4:12], lp[h, z, 36:44]))
            w[h, z, 4:8] = both[0:4]
            w[h, z, 40:44] = both[4:8]
        return carry

    lax.fori_loop(0, nz, invert_rim, 0)

    def faces_rim(z, carry):
        above = jnp.minimum(z + 1, nz - 1)
        top = jnp.where(z < nz - 1, 2.0, 0.0)
        mids = [jnp.where(sub < 4, w[h, z, 4:12], w[h, z, 35:43]) for h in range(2)]
        moved = [roll(m, -1) for m in mids]
        moved[0] = jnp.where(lane == 127, moved[1], moved[0])
        for h in range(2):
            across = jnp.where(sub < 4, w[h, z, 5:13], w[h, z, 36:44])
            higher = jnp.where(sub < 4, w[h, above, 4:12], w[h, above, 35:43])
            for ref, value in (
                (tx, 2.0 / (mids[h] + across)),
                (ty, 2.0 / (mids[h] + moved[h])),
                (tz, top / (mids[h] + higher)),
            ):
                ref[h, z, 4:8] = value[0:4]
                ref[h, z, 39:43] = value[4:8]
        return carry

    lax.fori_loop(0, nz, faces_rim, 0)

    moments = []
    for k in range(4):
        src, dst = fields[k], fields[k + 1]
        tiles = WIDE if k < 3 else OWN

        def layer(z, carry, k=k, src=src, dst=dst, tiles=tiles):
            sums, below = carry
            above = jnp.minimum(z + 1, nz - 1)
            turn = lax.rem(120 - 16 * (z // zp_count) + 128, 128)
            sums, below, after = list(sums), list(below), []
            for n, r in enumerate(tiles):
                rows = slice(r, r + 8)
                up, down = slice(r + 1, r + 9), slice(r - 1, r + 7)
                side = roll(q[k, lax.rem(z, zp_count), rows], turn)
                v = [src[h, z, rows] for h in range(2)]
                moved = [roll(v[h], -1) for h in range(2)]
                moved[0] = jnp.where(lane == 127, moved[1], moved[0])
                fy = [ty[h, z, rows] * (v[h] - moved[h]) for h in range(2)]
                fy[1] = jnp.where(lane == 127, side, fy[1])
                back = [roll(fy[h], 1) for h in range(2)]
                back[1] = jnp.where(lane == 0, back[0], back[1])
                back[0] = jnp.where(lane == 0, side, back[0])
                for h in range(2):
                    fz = tz[h, z, rows] * (v[h] - src[h, above, rows])
                    total = tx[h, z, rows] * (v[h] - src[h, z, up])
                    total = total + tx[h, z, down] * (v[h] - src[h, z, down])
                    total = total + (fy[h] - back[h]) + (fz - below[2 * n + h])
                    after.append(fz)
                    mine, new = v[h], total
                    if r == 4:
                        total = jnp.where(keep_top, total, 0.0)
                        mine = jnp.where(sub >= 4, mine, 0.0)
                        new = jnp.where(sub >= 4, total, 0.0)
                    if r == 36:
                        total = jnp.where(keep_bottom, total, 0.0)
                        mine = jnp.where(sub < 4, mine, 0.0)
                        new = jnp.where(sub < 4, total, 0.0)
                    dst[h, z, rows] = total
                    if k == 0:
                        sums[2] = sums[2] + mine * mine
                    sums[0] = sums[0] + mine * new
                    if k < 3:
                        sums[1] = sums[1] + new * new
            return tuple(sums), tuple(after)

        zero = jnp.zeros((8, 128), F32)
        count = 3 if k == 0 else 2 if k < 3 else 1
        sums, _ = lax.fori_loop(0, nz, layer, ((zero,) * count, (zero,) * (2 * len(tiles))))
        if k == 0:
            moments.append(sums[2])
        moments.extend(sums[:2])

    row = jnp.zeros((8, 128), F32)
    for n, part in enumerate(moments):
        row = jnp.where(lane == n, jnp.sum(part, axis=1, keepdims=True), row)
    row = jnp.sum(row, axis=0, keepdims=True)

    def exchange(value, slot, red, count, send, recv, where):
        send_row[slot:slot + 1, :] = value
        red[0:1, :] = value
        copies = []
        for d in range(1, count):
            copies.append(pltpu.make_async_remote_copy(
                src_ref=send_row.at[pl.ds(slot, 1), :],
                dst_ref=red.at[pl.ds(count - d, 1), :],
                send_sem=send.at[d],
                recv_sem=recv.at[count - d],
                device_id=where(d),
                device_id_type=MESH,
            ))
        for copy in copies:
            copy.start()
        for copy in copies:
            copy.wait_recv()
        return copies

    sent = exchange(row, 0, red_a, gx, a_send, a_recv, lambda d: (lax.rem(i + d, gx), j))
    part = red_a[...]
    hi, lo = tree(part, jnp.zeros_like(part))
    row = jnp.where(lane < 8, hi, pltpu.roll(lo, 8, 1))[0:1]
    sent += exchange(row, 8, red_b, gy, c_send, c_recv, lambda d: (i, lax.rem(j + d, gy)))
    parts = []
    for r in range(0, red_b.shape[0], 8):
        part = red_b[r:r + 8]
        parts.append((part, pltpu.roll(part, 120, 1)))
    total = parts[0]
    for part in parts[1:]:
        total = pair_add(total, part)
    hi, lo = tree(*total)
    splat = [
        (jnp.broadcast_to(hi[:, n:n + 1], (8, 128)), jnp.broadcast_to(lo[:, n:n + 1], (8, 128)))
        for n in range(8)
    ]
    for n, value in enumerate(coefficients(splat)):
        coef[n] = value

    for copy in sent:
        copy.wait_send()
    for di, dj, copy in s_copies:
        @pl.when(inside(di, dj))
        def _():
            copy.wait_send()
    for step, group in x_copies:
        @pl.when(inside(step, 0))
        def _():
            for copy in group:
                copy.wait_send()


def finish(nz, v0, v1, v2, v3, v4, tx, ty, q, coef, p_out, r_out, e_out, n_out,
           p_buf, r_buf, e_buf, n_buf, wide, side, sems):
    zp_count = nz // 8
    chunk = nz // 4
    lane = iota(1)
    c = [coef[n] for n in range(4)]

    def combine(parts):
        return (c[0] * parts[0] + c[1] * parts[1]) + (c[2] * parts[2] + c[3] * parts[3])

    for zp in range(zp_count):
        for r in OWN:
            side[zp, r:r + 8] = combine([q[k, zp, r:r + 8] for k in range(4)])

    def layer(z, carry):
        turn = lax.rem(120 - 16 * (z // zp_count) + 128, 128)
        press = {}
        for r in OWN:
            for h in range(2):
                v = [f[h, z, r:r + 8] for f in (v0, v1, v2, v3)]
                press[h, r] = combine(v)
                wide[h, r:r + 8] = press[h, r]
                cols = slice(128 * h, 128 * h + 128)
                p_buf[z, r - 8:r, cols] = press[h, r]
                r_buf[z, r - 8:r, cols] = v[0] - combine(v[1:] + [v4[h, z, r:r + 8]])
        for h in range(2):
            wide[h, 40:48] = combine([f[h, z, 40:48] for f in (v0, v1, v2, v3)])
        for r in OWN:
            moved = [roll(press[h, r], -1) for h in range(2)]
            moved[0] = jnp.where(lane == 127, moved[1], moved[0])
            for h in range(2):
                cols = slice(128 * h, 128 * h + 128)
                e_buf[z, r - 8:r, cols] = tx[h, z, r:r + 8] * (press[h, r] - wide[h, r + 1:r + 9])
                north = ty[h, z, r:r + 8] * (press[h, r] - moved[h])
                if h == 1:
                    north = jnp.where(lane == 127, roll(side[lax.rem(z, zp_count), r:r + 8], turn), north)
                n_buf[z, r - 8:r, cols] = north
        return carry

    copies = []
    for part in range(4):
        lax.fori_loop(part * chunk, (part + 1) * chunk, layer, 0)
        for n, (buf, out) in enumerate(((p_buf, p_out), (r_buf, r_out), (e_buf, e_out), (n_buf, n_out))):
            copy = pltpu.make_async_copy(
                buf.at[pl.ds(part * chunk, chunk)],
                out.at[0, pl.ds(part * chunk, chunk)],
                sems.at[4 * part + n],
            )
            copy.start()
            copies.append(copy)
    for copy in copies:
        copy.wait()


def solution(mesh):
    gx, gy = mesh.shape["gx"], mesh.shape["gy"]

    def on_device(log_perm, source):
        nz = log_perm.shape[1]
        zp = nz // 8
        field = (2, nz, ROWS, 128)
        strip = (zp, ROWS, 128)
        vmem = pl.BlockSpec(memory_space=pltpu.VMEM)
        hbm = pl.BlockSpec(memory_space=pltpu.HBM)
        made = pl.pallas_call(
            functools.partial(build, nz, gx, gy),
            out_shape=[pltpu.VMEM(field, F32)] * 7 + [pltpu.VMEM((4,) + strip, F32), pltpu.VMEM((4, 8, 128), F32)],
            in_specs=[hbm] * 2,
            out_specs=[vmem] * 9,
            scratch_shapes=[pltpu.VMEM(field, F32)] * 3
            + [pltpu.VMEM(strip, F32)] * 12
            + [
                pltpu.VMEM((16, 128), F32),
                pltpu.VMEM((8, 128), F32),
                pltpu.VMEM((max(8, gy), 128), F32),
                pltpu.SemaphoreType.DMA((4,)),
                pltpu.SemaphoreType.DMA((8,)),
                pltpu.SemaphoreType.DMA((8,)),
                pltpu.SemaphoreType.DMA((8,)),
                pltpu.SemaphoreType.DMA((8,)),
                pltpu.SemaphoreType.DMA((gx,)),
                pltpu.SemaphoreType.DMA((gx,)),
                pltpu.SemaphoreType.DMA((gy,)),
                pltpu.SemaphoreType.DMA((gy,)),
            ],
            compiler_params=pltpu.CompilerParams(
                collective_id=0, has_side_effects=True, vmem_limit_bytes=24 << 20
            ),
            name="build",
        )(*(pltpu.with_memory_space_constraint(x, pltpu.HBM) for x in (log_perm, source)))
        shape = jax.ShapeDtypeStruct(log_perm.shape, F32)
        return pl.pallas_call(
            functools.partial(finish, nz),
            out_shape=[shape] * 4,
            in_specs=[vmem] * 9,
            out_specs=[hbm] * 4,
            scratch_shapes=[pltpu.VMEM((nz, 32, 256), F32)] * 4
            + [pltpu.VMEM((2, ROWS, 128), F32), pltpu.VMEM(strip, F32), pltpu.SemaphoreType.DMA((16,))],
            compiler_params=pltpu.CompilerParams(vmem_limit_bytes=24 << 20),
            name="finish",
        )(*made)

    spec = P(None, None, "gx", "gy")
    return jax.shard_map(
        on_device, mesh=mesh, in_specs=(spec, spec), out_specs=(spec,) * 4, check_vma=False
    )
```

time: 480 us -> 52.6 us (0.11)
  the two profiles are of different devices: /device:TPU:12 before, /device:TPU:0 now
where the time goes in v1:
time: 52.6 us; the launch traced here: 52.5 us
  Pallas kernels  51.8 us (98%)
  between operations  0.64 us (1%)
    pallas_call x1, Pallas kernels, on_device(): pl.pallas_call(functools.partial(build, nz, gx, gy), out_shape=[pltpu.VME...  47.6 us
    pallas_call x1, Pallas kernels, on_device(): pl.pallas_call(functools.partial(finish, nz), out_shape=[shape] * 4, in_s...  4.28 us

profile of v1, /device:TPU:0, one launch (start us, length us, event | category | flops | bytes accessed | tf_op | source)
XLA Modules:
  0.0 52.5 jit_solution(11905482521925425063)
XLA Ops:
  0.6 47.6 %build.1 = (f32[2,32,48,128]{3,2,1,0:T(8,128)S(1)}, f32[2,32,48,128]{3,2,1,0:T(8,128)S(1)}, f32[2,32,48,128]{3,2,1,0:T(8,128)S(1)}, f32[2,32,48,128]{3,2,1,0:T(8...) custom-call(f32[1,32,32,256]{3,2,1,0:T(8,128)} %lp_ref.1, ...), custom_call_target="tpu_custom_call" | custom-call | tf_op jit(solution)/shard_map/build/pallas_call | solution.py:533
  48.2 4.3 %finish.1 = (f32[1,32,32,256]{3,2,1,0:T(8,128)}, f32[1,32,32,256]{3,2,1,0:T(8,128)}, f32[1,32,32,256]{3,2,1,0:T(8,128)}, f32[1,32,32,256]{3,2,1,0:T(8,128)}) custom-call(f32[2,32,48,128]{3,2,1,0:T(8,128)S(1)} %get-tuple-element.13.v0, f32[2,32,48,128]{3,2,1,0:T(8,128)S(1)} %get-tuple-element.14.v1, f32[2,32,48,128]{3,2,1,0:T(8,128)S(1)} %get-tuple-element.15.v2, ...), custom_call_target="tpu_custom_call" | custom-call | tf_op jit(solution)/shard_map/finish/pallas_call | solution.py:560

commit v2 on v1

--- a/solution.py
+++ b/solution.py
@@ -13,6 +13,8 @@
 ROWS = 48
 WIDE = (4, 12, 20, 28, 36)
 OWN = (8, 16, 24, 32)
+PARTS = 4
+BLOCK = 4
 DIRS = ((0, 1), (0, -1), (1, 0), (-1, 0), (1, 1), (1, -1), (-1, 1), (-1, -1))
 
 
@@ -96,28 +98,30 @@
     return x
 
 
+def shifted(pair):
+    lane = iota(1)
+    right = [roll(p, -1) for p in pair]
+    left = [roll(p, 1) for p in pair]
+    right[0] = jnp.where(lane == 127, right[1], right[0])
+    left[1] = jnp.where(lane == 0, left[0], left[1])
+    return right, left
+
+
 def tree(hi, lo):
     for shift in (4, 2, 1):
         hi, lo = pair_add((hi, lo), (pltpu.roll(hi, shift, 0), pltpu.roll(lo, shift, 0)))
     return hi, lo
 
 
-def build(nz, gx, gy, lp_ref, src_ref, v0, v1, v2, v3, v4, tx, ty, q, coef,
-          lp, w, tz, s_own, s_left, s_right, ws, txs, tys, tzs, b0, b1, b2, b3, fzs,
-          send_row, red_a, red_b, load_sem, x_send, x_recv, s_send, s_recv, a_send, a_recv, c_send, c_recv):
+def gather(nz, gx, gy, lp_ref, src_ref, v0, tx, ty, tz, tym, yp, ym, q,
+           lp, w, s_own, s_left, s_right, ws, txs, tys, tzs, b0, b1, b2, b3, fzs,
+           load_sem, x_send, x_recv, s_send, s_recv):
     i = lax.axis_index("gx")
     j = lax.axis_index("gy")
     zp_count = nz // 8
-    fields = (v0, v1, v2, v3, v4)
     strips = (b0, b1, b2, b3)
     lane, sub = iota(1), iota(0)
     l16 = lane % 16
-
-    barrier = pltpu.get_barrier_semaphore()
-    for d in range(1, gx):
-        pl.semaphore_signal(barrier, inc=1, device_id=(lax.rem(i + d, gx), j), device_id_type=MESH)
-    for d in range(1, gy):
-        pl.semaphore_signal(barrier, inc=1, device_id=(i, lax.rem(j + d, gy)), device_id_type=MESH)
 
     def inside(di, dj):
         ok = None
@@ -127,7 +131,8 @@
             ok = cond if ok is None else jnp.logical_and(ok, cond)
         return ok
 
-    for di, dj in DIRS[4:]:
+    barrier = pltpu.get_barrier_semaphore()
+    for di, dj in DIRS:
         @pl.when(inside(di, dj))
         def _():
             pl.semaphore_signal(barrier, inc=1, device_id=(i + di, j + dj), device_id_type=MESH)
@@ -178,13 +183,9 @@
                 for r in OWN:
                     buf[zp, r:r + 8] = jnp.zeros((8, 128), F32)
 
-    for n, red in ((gx, red_a), (gy, red_b)):
-        for r in range(n, red.shape[0]):
-            red[r:r + 1, :] = jnp.zeros((1, 128), F32)
-
     inner_i = (i > 0).astype(jnp.int32) + (i < gx - 1).astype(jnp.int32)
     inner_j = (j > 0).astype(jnp.int32) + (j < gy - 1).astype(jnp.int32)
-    pl.semaphore_wait(barrier, gx - 1 + gy - 1 + inner_i * inner_j)
+    pl.semaphore_wait(barrier, inner_i + inner_j + inner_i * inner_j)
 
     x_copies = []
     for step, first, land in ((1, 28, 4), (-1, 0, 40)):
@@ -260,13 +261,16 @@
         above = jnp.minimum(z + 1, nz - 1)
         top = jnp.where(z < nz - 1, 2.0, 0.0)
         for r in OWN:
-            w0, w1 = w[0, z, r:r + 8], w[1, z, r:r + 8]
-            n0, n1 = roll(w0, -1), roll(w1, -1)
-            ty[0, z, r:r + 8] = 2.0 / (w0 + jnp.where(lane == 127, n1, n0))
-            ty[1, z, r:r + 8] = 2.0 / (w1 + n1)
-            for h, mid in ((0, w0), (1, w1)):
+            mids = [w[h, z, r:r + 8] for h in range(2)]
+            right, left = shifted(mids)
+            more, less = shifted([v0[h, z, r:r + 8] for h in range(2)])
+            for h, mid in enumerate(mids):
+                ty[h, z, r:r + 8] = 2.0 / (mid + right[h])
+                tym[h, z, r:r + 8] = 2.0 / (mid + left[h])
                 tx[h, z, r:r + 8] = 2.0 / (mid + w[h, z, r + 1:r + 9])
                 tz[h, z, r:r + 8] = top / (mid + w[h, above, r:r + 8])
+                yp[h, z, r:r + 8] = more[h]
+                ym[h, z, r:r + 8] = less[h]
         return carry
 
     lax.fori_loop(0, nz, faces, 0)
@@ -328,83 +332,156 @@
             for copy in group:
                 copy.wait_recv()
 
-    def invert_rim(z, carry):
-        for h in range(2):
-            both = jnp.exp(-jnp.where(sub < 4, lp[h, z, 4:12], lp[h, z, 36:44]))
-            w[h, z, 4:8] = both[0:4]
-            w[h, z, 40:44] = both[4:8]
+    def invert_rim(step, carry):
+        for u in range(BLOCK):
+            z = BLOCK * step + u
+            for h in range(2):
+                both = jnp.exp(-jnp.where(sub < 4, lp[h, z, 4:12], lp[h, z, 36:44]))
+                w[h, z, 4:8] = both[0:4]
+                w[h, z, 40:44] = both[4:8]
         return carry
 
-    lax.fori_loop(0, nz, invert_rim, 0)
-
-    def faces_rim(z, carry):
-        above = jnp.minimum(z + 1, nz - 1)
-        top = jnp.where(z < nz - 1, 2.0, 0.0)
-        mids = [jnp.where(sub < 4, w[h, z, 4:12], w[h, z, 35:43]) for h in range(2)]
-        moved = [roll(m, -1) for m in mids]
-        moved[0] = jnp.where(lane == 127, moved[1], moved[0])
-        for h in range(2):
-            across = jnp.where(sub < 4, w[h, z, 5:13], w[h, z, 36:44])
-            higher = jnp.where(sub < 4, w[h, above, 4:12], w[h, above, 35:43])
-            for ref, value in (
-                (tx, 2.0 / (mids[h] + across)),
-                (ty, 2.0 / (mids[h] + moved[h])),
-                (tz, top / (mids[h] + higher)),
-            ):
-                ref[h, z, 4:8] = value[0:4]
-                ref[h, z, 39:43] = value[4:8]
+    lax.fori_loop(0, nz // BLOCK, invert_rim, 0)
+
+    def faces_rim(step, carry):
+        layers = []
+        for u in range(BLOCK):
+            z = BLOCK * step + u
+            mids = [jnp.where(sub < 4, w[h, z, 4:12], w[h, z, 35:43]) for h in range(2)]
+            edge = [jnp.where(sub < 4, v0[h, z, 4:12], v0[h, z, 36:44]) for h in range(2)]
+            layers.append((z, mids, shifted(mids), shifted(edge)))
+        for z, mids, (right, left), (more, less) in layers:
+            above = jnp.minimum(z + 1, nz - 1)
+            top = jnp.where(z < nz - 1, 2.0, 0.0)
+            for h, mid in enumerate(mids):
+                across = jnp.where(sub < 4, w[h, z, 5:13], w[h, z, 36:44])
+                higher = jnp.where(sub < 4, w[h, above, 4:12], w[h, above, 35:43])
+                for ref, value in (
+                    (tx, 2.0 / (mid + across)),
+                    (ty, 2.0 / (mid + right[h])),
+                    (tym, 2.0 / (mid + left[h])),
+                    (tz, top / (mid + higher)),
+                ):
+                    ref[h, z, 4:8] = value[0:4]
+                    ref[h, z, 39:43] = value[4:8]
+                for ref, value in ((yp, more[h]), (ym, less[h])):
+                    ref[h, z, 4:8] = value[0:4]
+                    ref[h, z, 40:44] = value[4:8]
         return carry
 
-    lax.fori_loop(0, nz, faces_rim, 0)
+    lax.fori_loop(0, nz // BLOCK, faces_rim, 0)
+
+    for di, dj, copy in s_copies:
+        @pl.when(inside(di, dj))
+        def _():
+            copy.wait_send()
+    for step, group in x_copies:
+        @pl.when(inside(step, 0))
+        def _():
+            for copy in group:
+                copy.wait_send()
+
+
+def powers(nz, gx, gy, v0, tx, ty, tz, tym, yp0, ym0, q, v1, v2, v3, v4, coef,
+           yp1, ym1, yp2, ym2, sides, send_row, red_a, red_b, a_send, a_recv, c_send, c_recv):
+    i = lax.axis_index("gx")
+    j = lax.axis_index("gy")
+    zp_count = nz // 8
+    fields = (v0, v1, v2, v3, v4)
+    lane, sub = iota(1), iota(0)
+    keep_top = jnp.logical_or(sub >= 4, i > 0)
+    keep_bottom = jnp.logical_or(sub < 4, i < gx - 1)
+
+    barrier = pltpu.get_barrier_semaphore()
+    for d in range(1, gx):
+        pl.semaphore_signal(barrier, inc=1, device_id=(lax.rem(i + d, gx), j), device_id_type=MESH)
+    for d in range(1, gy):
+        pl.semaphore_signal(barrier, inc=1, device_id=(i, lax.rem(j + d, gy)), device_id_type=MESH)
+    for n, red in ((gx, red_a), (gy, red_b)):
+        for r in range(n, red.shape[0]):
+            red[r:r + 1, :] = jnp.zeros((1, 128), F32)
+
+
+    steps = nz // BLOCK
+
+    def turned(k, z, r):
+        turn = lax.rem(248 - 16 * (z // zp_count), 128)
+        return roll(q[k, lax.rem(z, zp_count), r:r + 8], turn)
 
     moments = []
     for k in range(4):
         src, dst = fields[k], fields[k + 1]
         tiles = WIDE if k < 3 else OWN
-
-        def layer(z, carry, k=k, src=src, dst=dst, tiles=tiles):
-            sums, below = carry
-            above = jnp.minimum(z + 1, nz - 1)
-            turn = lax.rem(120 - 16 * (z // zp_count) + 128, 128)
-            sums, below, after = list(sums), list(below), []
+        for u in range(BLOCK):
             for n, r in enumerate(tiles):
-                rows = slice(r, r + 8)
-                up, down = slice(r + 1, r + 9), slice(r - 1, r + 7)
-                side = roll(q[k, lax.rem(z, zp_count), rows], turn)
-                v = [src[h, z, rows] for h in range(2)]
-                moved = [roll(v[h], -1) for h in range(2)]
-                moved[0] = jnp.where(lane == 127, moved[1], moved[0])
-                fy = [ty[h, z, rows] * (v[h] - moved[h]) for h in range(2)]
-                fy[1] = jnp.where(lane == 127, side, fy[1])
-                back = [roll(fy[h], 1) for h in range(2)]
-                back[1] = jnp.where(lane == 0, back[0], back[1])
-                back[0] = jnp.where(lane == 0, side, back[0])
+                sides[0, u, n] = turned(k, u, r)
+
+        def spread(z, dst=dst):
+            return [shifted([dst[h, z, r:r + 8] for h in range(2)]) for r in WIDE]
+
+        def settle(z, moved, k=k):
+            yp, ym = (yp2, ym2) if k == 1 else (yp1, ym1)
+            for r, (right, left) in zip(WIDE, moved):
                 for h in range(2):
-                    fz = tz[h, z, rows] * (v[h] - src[h, above, rows])
-                    total = tx[h, z, rows] * (v[h] - src[h, z, up])
-                    total = total + tx[h, z, down] * (v[h] - src[h, z, down])
-                    total = total + (fy[h] - back[h]) + (fz - below[2 * n + h])
-                    after.append(fz)
-                    mine, new = v[h], total
-                    if r == 4:
-                        total = jnp.where(keep_top, total, 0.0)
-                        mine = jnp.where(sub >= 4, mine, 0.0)
-                        new = jnp.where(sub >= 4, total, 0.0)
-                    if r == 36:
-                        total = jnp.where(keep_bottom, total, 0.0)
-                        mine = jnp.where(sub < 4, mine, 0.0)
-                        new = jnp.where(sub < 4, total, 0.0)
-                    dst[h, z, rows] = total
-                    if k == 0:
-                        sums[2] = sums[2] + mine * mine
-                    sums[0] = sums[0] + mine * new
-                    if k < 3:
-                        sums[1] = sums[1] + new * new
-            return tuple(sums), tuple(after)
+                    yp[h, z, r:r + 8] = right[h]
+                    ym[h, z, r:r + 8] = left[h]
+
+        def block(step, carry, k=k, src=src, dst=dst, tiles=tiles, spread=spread, settle=settle):
+            sums, below = list(carry[0]), list(carry[1])
+            after, before = ((yp0, ym0), (yp1, ym1), (yp2, ym2), (yp1, ym1))[k]
+            now = lax.rem(step, 2)
+            moved = {}
+            for u in range(BLOCK):
+                z = BLOCK * step + u
+                last = jnp.maximum(z - BLOCK, u)
+                later = jnp.minimum(z + BLOCK, nz - BLOCK + u)
+                if k < 3:
+                    moved = spread(last)
+                fresh = [turned(k, later, r) for r in tiles]
+                above = jnp.minimum(z + 1, nz - 1)
+                for n, r in enumerate(tiles):
+                    rows, up, down = slice(r, r + 8), slice(r + 1, r + 9), slice(r - 1, r + 7)
+                    side = sides[now, u, n]
+                    for h in range(2):
+                        v = src[h, z, rows]
+                        ahead = ty[h, z, rows] * (v - after[h, z, rows])
+                        back = tym[h, z, rows] * (v - before[h, z, rows])
+                        if h == 0:
+                            back = jnp.where(lane == 0, -side, back)
+                        else:
+                            ahead = jnp.where(lane == 127, side, ahead)
+                        fz = tz[h, z, rows] * (v - src[h, above, rows])
+                        total = tx[h, z, rows] * (v - src[h, z, up])
+                        total = total + tx[h, z, down] * (v - src[h, z, down])
+                        total = total + (ahead + back) + (fz - below[2 * n + h])
+                        below[2 * n + h] = fz
+                        mine, new = v, total
+                        if r == 4:
+                            total = jnp.where(keep_top, total, 0.0)
+                            mine = jnp.where(sub >= 4, mine, 0.0)
+                            new = jnp.where(sub >= 4, total, 0.0)
+                        if r == 36:
+                            total = jnp.where(keep_bottom, total, 0.0)
+                            mine = jnp.where(sub < 4, mine, 0.0)
+                            new = jnp.where(sub < 4, total, 0.0)
+                        dst[h, z, rows] = total
+                        if k == 0:
+                            sums[2] = sums[2] + mine * mine
+                        sums[0] = sums[0] + mine * new
+                        if k < 3:
+                            sums[1] = sums[1] + new * new
+                for n in range(len(tiles)):
+                    sides[1 - now, u, n] = fresh[n]
+                if k < 3:
+                    settle(last, moved)
+            return tuple(sums), tuple(below)
 
         zero = jnp.zeros((8, 128), F32)
         count = 3 if k == 0 else 2 if k < 3 else 1
-        sums, _ = lax.fori_loop(0, nz, layer, ((zero,) * count, (zero,) * (2 * len(tiles))))
+        sums, _ = lax.fori_loop(0, steps, block, ((zero,) * count, (zero,) * (2 * len(tiles))))
+        if k < 3:
+            for u in range(BLOCK):
+                settle(nz - BLOCK + u, spread(nz - BLOCK + u))
         if k == 0:
             moments.append(sums[2])
         moments.extend(sums[:2])
@@ -433,6 +510,7 @@
             copy.wait_recv()
         return copies
 
+    pl.semaphore_wait(barrier, gx - 1 + gy - 1)
     sent = exchange(row, 0, red_a, gx, a_send, a_recv, lambda d: (lax.rem(i + d, gx), j))
     part = red_a[...]
     hi, lo = tree(part, jnp.zeros_like(part))
@@ -455,21 +533,12 @@
 
     for copy in sent:
         copy.wait_send()
-    for di, dj, copy in s_copies:
-        @pl.when(inside(di, dj))
-        def _():
-            copy.wait_send()
-    for step, group in x_copies:
-        @pl.when(inside(step, 0))
-        def _():
-            for copy in group:
-                copy.wait_send()
 
 
 def finish(nz, v0, v1, v2, v3, v4, tx, ty, q, coef, p_out, r_out, e_out, n_out,
            p_buf, r_buf, e_buf, n_buf, wide, side, sems):
     zp_count = nz // 8
-    chunk = nz // 4
+    chunk = nz // PARTS
     lane = iota(1)
     c = [coef[n] for n in range(4)]
 
@@ -480,34 +549,49 @@
         for r in OWN:
             side[zp, r:r + 8] = combine([q[k, zp, r:r + 8] for k in range(4)])
 
-    def layer(z, carry):
-        turn = lax.rem(120 - 16 * (z // zp_count) + 128, 128)
-        press = {}
-        for r in OWN:
+    def block(step, carry):
+        moved = {}
+
+        def first(u):
+            z = BLOCK * step + u
+            turn = lax.rem(248 - 16 * (z // zp_count), 128)
+            for r in OWN:
+                press = []
+                for h in range(2):
+                    v = [f[h, z, r:r + 8] for f in (v0, v1, v2, v3)]
+                    press.append(combine(v))
+                    wide[u, h, r:r + 8] = press[h]
+                    cols = slice(128 * h, 128 * h + 128)
+                    p_buf[z, r - 8:r, cols] = press[h]
+                    r_buf[z, r - 8:r, cols] = v[0] - combine(v[1:] + [v4[h, z, r:r + 8]])
+                moved[u, r] = [roll(p, -1) for p in press]
+                moved[u, r].append(roll(side[lax.rem(z, zp_count), r:r + 8], turn))
             for h in range(2):
-                v = [f[h, z, r:r + 8] for f in (v0, v1, v2, v3)]
-                press[h, r] = combine(v)
-                wide[h, r:r + 8] = press[h, r]
-                cols = slice(128 * h, 128 * h + 128)
-                p_buf[z, r - 8:r, cols] = press[h, r]
-                r_buf[z, r - 8:r, cols] = v[0] - combine(v[1:] + [v4[h, z, r:r + 8]])
-        for h in range(2):
-            wide[h, 40:48] = combine([f[h, z, 40:48] for f in (v0, v1, v2, v3)])
-        for r in OWN:
-            moved = [roll(press[h, r], -1) for h in range(2)]
-            moved[0] = jnp.where(lane == 127, moved[1], moved[0])
-            for h in range(2):
-                cols = slice(128 * h, 128 * h + 128)
-                e_buf[z, r - 8:r, cols] = tx[h, z, r:r + 8] * (press[h, r] - wide[h, r + 1:r + 9])
-                north = ty[h, z, r:r + 8] * (press[h, r] - moved[h])
-                if h == 1:
-                    north = jnp.where(lane == 127, roll(side[lax.rem(z, zp_count), r:r + 8], turn), north)
-                n_buf[z, r - 8:r, cols] = north
+                wide[u, h, 40:48] = combine([f[h, z, 40:48] for f in (v0, v1, v2, v3)])
+
+        def second(u):
+            z = BLOCK * step + u
+            for r in OWN:
+                one, two, rim = moved[u, r]
+                for h, across in ((0, jnp.where(lane == 127, two, one)), (1, two)):
+                    cols = slice(128 * h, 128 * h + 128)
+                    press = wide[u, h, r:r + 8]
+                    e_buf[z, r - 8:r, cols] = tx[h, z, r:r + 8] * (press - wide[u, h, r + 1:r + 9])
+                    north = ty[h, z, r:r + 8] * (press - across)
+                    if h == 1:
+                        north = jnp.where(lane == 127, rim, north)
+                    n_buf[z, r - 8:r, cols] = north
+
+        for u in range(BLOCK):
+            first(u)
+            if u:
+                second(u - 1)
+        second(BLOCK - 1)
         return carry
 
     copies = []
-    for part in range(4):
-        lax.fori_loop(part * chunk, (part + 1) * chunk, layer, 0)
+    for part in range(PARTS):
+        lax.fori_loop(part * chunk // BLOCK, (part + 1) * chunk // BLOCK, block, 0)
         for n, (buf, out) in enumerate(((p_buf, p_out), (r_buf, r_out), (e_buf, e_out), (n_buf, n_out))):
             copy = pltpu.make_async_copy(
                 buf.at[pl.ds(part * chunk, chunk)],
@@ -531,31 +615,39 @@
         vmem = pl.BlockSpec(memory_space=pltpu.VMEM)
         hbm = pl.BlockSpec(memory_space=pltpu.HBM)
         made = pl.pallas_call(
-            functools.partial(build, nz, gx, gy),
-            out_shape=[pltpu.VMEM(field, F32)] * 7 + [pltpu.VMEM((4,) + strip, F32), pltpu.VMEM((4, 8, 128), F32)],
+            functools.partial(gather, nz, gx, gy),
+            out_shape=[pltpu.VMEM(field, F32)] * 7 + [pltpu.VMEM((4,) + strip, F32)],
             in_specs=[hbm] * 2,
-            out_specs=[vmem] * 9,
-            scratch_shapes=[pltpu.VMEM(field, F32)] * 3
+            out_specs=[vmem] * 8,
+            scratch_shapes=[pltpu.VMEM(field, F32)] * 2
             + [pltpu.VMEM(strip, F32)] * 12
+            + [pltpu.SemaphoreType.DMA((4,))]
+            + [pltpu.SemaphoreType.DMA((8,))] * 4,
+            compiler_params=pltpu.CompilerParams(
+                collective_id=0, has_side_effects=True, vmem_limit_bytes=16 << 20
+            ),
+            name="gather",
+        )(*(pltpu.with_memory_space_constraint(x, pltpu.HBM) for x in (log_perm, source)))
+        v0, tx, ty, tz, tym, yp, ym, q = made
+        v1, v2, v3, v4, coef = pl.pallas_call(
+            functools.partial(powers, nz, gx, gy),
+            out_shape=[pltpu.VMEM(field, F32)] * 4 + [pltpu.VMEM((4, 8, 128), F32)],
+            in_specs=[vmem] * 8,
+            out_specs=[vmem] * 5,
+            scratch_shapes=[pltpu.VMEM(field, F32)] * 4
             + [
+                pltpu.VMEM((2, BLOCK, 5, 8, 128), F32),
                 pltpu.VMEM((16, 128), F32),
                 pltpu.VMEM((8, 128), F32),
                 pltpu.VMEM((max(8, gy), 128), F32),
-                pltpu.SemaphoreType.DMA((4,)),
-                pltpu.SemaphoreType.DMA((8,)),
-                pltpu.SemaphoreType.DMA((8,)),
-                pltpu.SemaphoreType.DMA((8,)),
-                pltpu.SemaphoreType.DMA((8,)),
-                pltpu.SemaphoreType.DMA((gx,)),
-                pltpu.SemaphoreType.DMA((gx,)),
-                pltpu.SemaphoreType.DMA((gy,)),
-                pltpu.SemaphoreType.DMA((gy,)),
-            ],
+            ]
+            + [pltpu.SemaphoreType.DMA((gx,))] * 2
+            + [pltpu.SemaphoreType.DMA((gy,))] * 2,
             compiler_params=pltpu.CompilerParams(
-                collective_id=0, has_side_effects=True, vmem_limit_bytes=24 << 20
+                collective_id=1, has_side_effects=True, vmem_limit_bytes=14 << 20
             ),
-            name="build",
-        )(*(pltpu.with_memory_space_constraint(x, pltpu.HBM) for x in (log_perm, source)))
+            name="powers",
+        )(*made)
         shape = jax.ShapeDtypeStruct(log_perm.shape, F32)
         return pl.pallas_call(
             functools.partial(finish, nz),
@@ -563,10 +655,10 @@
             in_specs=[vmem] * 9,
             out_specs=[hbm] * 4,
             scratch_shapes=[pltpu.VMEM((nz, 32, 256), F32)] * 4
-            + [pltpu.VMEM((2, ROWS, 128), F32), pltpu.VMEM(strip, F32), pltpu.SemaphoreType.DMA((16,))],
-            compiler_params=pltpu.CompilerParams(vmem_limit_bytes=24 << 20),
+            + [pltpu.VMEM((BLOCK, 2, ROWS, 128), F32), pltpu.VMEM(strip, F32), pltpu.SemaphoreType.DMA((4 * PARTS,))],
+            compiler_params=pltpu.CompilerParams(vmem_limit_bytes=12 << 20),
             name="finish",
-        )(*made)
+        )(v0, v1, v2, v3, v4, tx, ty, q, coef)
 
     spec = P(None, None, "gx", "gy")
     return jax.shard_map(

time: 52.6 us -> 34.5 us (0.66)
  Pallas kernels: 51.8 us -> 33.7 us
    pallas_call x1 -> x2, Pallas kernels: 47.6 us -> 31.3 us  [the longest x1 22 us: on_device(): pl.pallas_call(functools.partial(powers, nz, gx, gy), out_shape=[pltpu.VM...]
    pallas_call x1, Pallas kernels: 4.28 us -> 2.41 us  [on_device(): pl.pallas_call(functools.partial(finish, nz), out_shape=[shape] * 4, in_s...]
where the time goes in v2:
time: 34.5 us; the launch traced here: 34.4 us
  Pallas kernels  33.7 us (98%)
  between operations  0.65 us (2%)
    pallas_call x1, Pallas kernels, on_device(): pl.pallas_call(functools.partial(powers, nz, gx, gy), out_shape=[pltpu.VM...  22 us
    pallas_call x1, Pallas kernels, on_device(): pl.pallas_call(functools.partial(gather, nz, gx, gy), out_shape=[pltpu.VM...  9.31 us
    pallas_call x1, Pallas kernels, on_device(): pl.pallas_call(functools.partial(finish, nz), out_shape=[shape] * 4, in_s...  2.41 us

profile of v2, /device:TPU:0, one launch (start us, length us, event | category | flops | bytes accessed | tf_op | source)
XLA Modules:
  0.0 34.4 jit_solution(865174945048772853)
XLA Ops:
  0.6 9.3 %gather.1 = (f32[2,32,48,128]{3,2,1,0:T(8,128)S(1)}, f32[2,32,48,128]{3,2,1,0:T(8,128)S(1)}, f32[2,32,48,128]{3,2,1,0:T(8,128)S(1)}, f32[2,32,48,128]{3,2,1,0:T(...) custom-call(f32[1,32,32,256]{3,2,1,0:T(8,128)} %lp_ref.1, ...), custom_call_target="tpu_custom_call" | custom-call | tf_op jit(solution)/shard_map/gather/pallas_call | solution.py:617
  9.9 22.0 %powers.1 = (f32[2,32,48,128]{3,2,1,0:T(8,128)S(1)}, f32[2,32,48,128]{3,2,1,0:T(8,128)S(1)}, f32[2,32,48,128]{3,2,1,0:T(8,128)S(1)}, f32[2,32,48,128]{3,2,1,0:T(8,128)S(1)}, f32[4,8,128]{2,1,0:T(8,128)S(1)}) custom-call(f32[2,32,48,128]{3,2,1,0:T(8,128)S(1)} %get-tuple-element.17.v0, f32[2,32,48,128]{3,2,1,0:T(8,128)S(1)} %get-tuple-element.18.tx, ...), custom_call_target="tpu_custom_call" | custom-call | tf_op jit(solution)/shard_map/powers/pallas_call | solution.py:632
  32.0 2.4 %finish.1 = (f32[1,32,32,256]{3,2,1,0:T(8,128)}, f32[1,32,32,256]{3,2,1,0:T(8,128)}, f32[1,32,32,256]{3,2,1,0:T(8,128)}, f32[1,32,32,256]{3,2,1,0:T(8,128)}) custom-call(f32[2,32,48,128]{3,2,1,0:T(8,128)S(1)} %get-tuple-element.17.v0, f32[2,32,48,128]{3,2,1,0:T(8,128)S(1)} %get-tuple-element.25.v1, f32[2,32,48,128]{3,2,1,0:T(8,128)S(1)} %get-tuple-element.26.v2, ...), custom_call_target="tpu_custom_call" | custom-call | tf_op jit(solution)/shard_map/finish/pallas_call | solution.py:652

commit v3 on v2

--- a/solution.py
+++ b/solution.py
@@ -114,14 +114,14 @@
 
 
 def gather(nz, gx, gy, lp_ref, src_ref, v0, tx, ty, tz, tym, yp, ym, q,
-           lp, w, s_own, s_left, s_right, ws, txs, tys, tzs, b0, b1, b2, b3, fzs,
+           lp, w, s_own, s_left, s_right, to_right, to_left, ws, txs, tys, tzs, b0, b1, b2, b3, fzs,
            load_sem, x_send, x_recv, s_send, s_recv):
     i = lax.axis_index("gx")
     j = lax.axis_index("gy")
     zp_count = nz // 8
     strips = (b0, b1, b2, b3)
     lane, sub = iota(1), iota(0)
-    l16 = lane % 16
+    l16, l8 = lane % 16, lane % 8
 
     def inside(di, dj):
         ok = None
@@ -130,12 +130,6 @@
         ) + ([] if dj == 0 else [j < gy - 1] if dj > 0 else [j > 0]):
             ok = cond if ok is None else jnp.logical_and(ok, cond)
         return ok
-
-    barrier = pltpu.get_barrier_semaphore()
-    for di, dj in DIRS:
-        @pl.when(inside(di, dj))
-        def _():
-            pl.semaphore_signal(barrier, inc=1, device_id=(i + di, j + dj), device_id_type=MESH)
 
     loads = []
     for n, (source, target) in enumerate(((src_ref, v0), (lp_ref, lp))):
@@ -148,6 +142,12 @@
             copy.start()
             loads.append(copy)
 
+    barrier = pltpu.get_barrier_semaphore()
+    for di, dj in DIRS:
+        @pl.when(inside(di, dj))
+        def _():
+            pl.semaphore_signal(barrier, inc=1, device_id=(i + di, j + dj), device_id_type=MESH)
+
     zero4 = jnp.zeros((4, 128), F32)
 
     @pl.when(i == 0)
@@ -158,8 +158,8 @@
                 lp[h, z, 4:8] = zero4
             return carry
         lax.fori_loop(0, nz, fill, 0)
-        for zp in range(zp_count):
-            for buf in (s_own, s_left, s_right):
+        for buf in (s_own, s_left, s_right):
+            for zp in range(buf.shape[0]):
                 buf[zp, 4:8] = zero4
 
     @pl.when(i == gx - 1)
@@ -170,14 +170,14 @@
                 lp[h, z, 40:44] = zero4
             return carry
         lax.fori_loop(0, nz, fill, 0)
-        for zp in range(zp_count):
-            for buf in (s_own, s_left, s_right):
+        for buf in (s_own, s_left, s_right):
+            for zp in range(buf.shape[0]):
                 buf[zp, 40:44] = zero4
 
     for edge, buf in ((j == 0, s_left), (j == gy - 1, s_right)):
         @pl.when(edge)
         def _():
-            for zp in range(zp_count):
+            for zp in range(zp_count // 2):
                 buf[zp, 4:8] = zero4
                 buf[zp, 40:44] = zero4
                 for r in OWN:
@@ -211,22 +211,28 @@
     for copy in loads:
         copy.wait()
 
-    def pack(zp, carry):
+    def pack(pair, carry):
         for r in OWN:
-            packed = jnp.zeros((8, 128), F32)
-            for g in range(8):
-                z = g * zp_count + zp
-                fld = jnp.where(lane < 64, v0[0, z, r:r + 8], v0[1, z, r:r + 8])
-                log = jnp.where(lane < 64, lp[0, z, r:r + 8], lp[1, z, r:r + 8])
-                both = jnp.where(l16 < 8, roll(log, 16 * g + 4), roll(fld, 16 * g + 12))
-                packed = jnp.where(lane // 16 == g, both, packed)
-            s_own[zp, r:r + 8] = packed
+            planes = []
+            for u in range(2):
+                packed = jnp.zeros((8, 128), F32)
+                for g in range(8):
+                    z = g * zp_count + 2 * pair + u
+                    fld = jnp.where(lane < 64, v0[0, z, r:r + 8], v0[1, z, r:r + 8])
+                    log = jnp.where(lane < 64, lp[0, z, r:r + 8], lp[1, z, r:r + 8])
+                    both = jnp.where(l16 < 8, roll(log, 16 * g + 4), roll(fld, 16 * g + 12))
+                    packed = jnp.where(lane // 16 == g, both, packed)
+                s_own[2 * pair + u, r:r + 8] = packed
+                planes.append(packed)
+            to_right[pair, r:r + 8] = jnp.where(l8 < 4, planes[0], roll(planes[1], 4))
+            to_left[pair, r:r + 8] = jnp.where(l8 < 4, roll(planes[1], -4), planes[0])
         return carry
 
-    lax.fori_loop(0, zp_count, pack, 0)
+    lax.fori_loop(0, zp_count // 2, pack, 0)
 
     s_copies = []
     for n, (di, dj) in enumerate(DIRS):
+        base = s_own if dj == 0 else to_right if dj > 0 else to_left
         target = s_own if dj == 0 else s_left if dj > 0 else s_right
         if di == 0:
             first, land, count = 8, 8, 32
@@ -235,7 +241,7 @@
         else:
             first, land, count = 8, 40, 4
         copy = pltpu.make_async_remote_copy(
-            src_ref=s_own.at[:, pl.ds(first, count), :],
+            src_ref=base.at[:, pl.ds(first, count), :],
             dst_ref=target.at[:, pl.ds(land, count), :],
             send_sem=s_send.at[n],
             recv_sem=s_recv.at[n],
@@ -249,31 +255,96 @@
         def _():
             copy.start()
 
-    def invert(z, carry):
-        for h in range(2):
+    def invert(step, carry):
+        for u in range(BLOCK):
+            for h in range(2):
+                for r in OWN:
+                    z = BLOCK * step + u
+                    w[h, z, r:r + 8] = jnp.exp(-lp[h, z, r:r + 8])
+        return carry
+
+    lax.fori_loop(0, nz // BLOCK, invert, 0)
+
+    def faces(step, carry):
+        for u in range(BLOCK):
+            z = BLOCK * step + u
+            above = jnp.minimum(z + 1, nz - 1)
+            top = jnp.where(z < nz - 1, 2.0, 0.0)
             for r in OWN:
-                w[h, z, r:r + 8] = jnp.exp(-lp[h, z, r:r + 8])
+                mids = [w[h, z, r:r + 8] for h in range(2)]
+                right, left = shifted(mids)
+                more, less = shifted([v0[h, z, r:r + 8] for h in range(2)])
+                for h, mid in enumerate(mids):
+                    ty[h, z, r:r + 8] = 2.0 / (mid + right[h])
+                    tym[h, z, r:r + 8] = 2.0 / (mid + left[h])
+                    tx[h, z, r:r + 8] = 2.0 / (mid + w[h, z, r + 1:r + 9])
+                    tz[h, z, r:r + 8] = top / (mid + w[h, above, r:r + 8])
+                    yp[h, z, r:r + 8] = more[h]
+                    ym[h, z, r:r + 8] = less[h]
         return carry
 
-    lax.fori_loop(0, nz, invert, 0)
-
-    def faces(z, carry):
-        above = jnp.minimum(z + 1, nz - 1)
-        top = jnp.where(z < nz - 1, 2.0, 0.0)
-        for r in OWN:
-            mids = [w[h, z, r:r + 8] for h in range(2)]
-            right, left = shifted(mids)
-            more, less = shifted([v0[h, z, r:r + 8] for h in range(2)])
+    lax.fori_loop(0, nz // BLOCK, faces, 0)
+
+    for step, group in x_copies:
+        @pl.when(inside(-step, 0))
+        def _():
+            for copy in group[:2]:
+                copy.wait_recv()
+
+    def invert_rim(step, carry):
+        for u in range(BLOCK):
+            z = BLOCK * step + u
+            for h in range(2):
+                both = jnp.exp(-jnp.where(sub < 4, lp[h, z, 4:12], lp[h, z, 36:44]))
+                w[h, z, 4:8] = both[0:4]
+                w[h, z, 40:44] = both[4:8]
+        return carry
+
+    lax.fori_loop(0, nz // BLOCK, invert_rim, 0)
+
+    def faces_rim(step, carry):
+        layers = []
+        for u in range(BLOCK):
+            z = BLOCK * step + u
+            mids = [jnp.where(sub < 4, w[h, z, 4:12], w[h, z, 35:43]) for h in range(2)]
+            layers.append((z, mids, shifted(mids)))
+        for z, mids, (right, left) in layers:
+            above = jnp.minimum(z + 1, nz - 1)
+            top = jnp.where(z < nz - 1, 2.0, 0.0)
             for h, mid in enumerate(mids):
-                ty[h, z, r:r + 8] = 2.0 / (mid + right[h])
-                tym[h, z, r:r + 8] = 2.0 / (mid + left[h])
-                tx[h, z, r:r + 8] = 2.0 / (mid + w[h, z, r + 1:r + 9])
-                tz[h, z, r:r + 8] = top / (mid + w[h, above, r:r + 8])
-                yp[h, z, r:r + 8] = more[h]
-                ym[h, z, r:r + 8] = less[h]
+                across = jnp.where(sub < 4, w[h, z, 5:13], w[h, z, 36:44])
+                higher = jnp.where(sub < 4, w[h, above, 4:12], w[h, above, 35:43])
+                for ref, value in (
+                    (tx, 2.0 / (mid + across)),
+                    (ty, 2.0 / (mid + right[h])),
+                    (tym, 2.0 / (mid + left[h])),
+                    (tz, top / (mid + higher)),
+                ):
+                    ref[h, z, 4:8] = value[0:4]
+                    ref[h, z, 39:43] = value[4:8]
         return carry
 
-    lax.fori_loop(0, nz, faces, 0)
+    lax.fori_loop(0, nz // BLOCK, faces_rim, 0)
+
+    for step, group in x_copies:
+        @pl.when(inside(-step, 0))
+        def _():
+            for copy in group[2:]:
+                copy.wait_recv()
+
+    def moved_rim(step, carry):
+        layers = []
+        for u in range(BLOCK):
+            z = BLOCK * step + u
+            layers.append((z, shifted([jnp.where(sub < 4, v0[h, z, 4:12], v0[h, z, 36:44]) for h in range(2)])))
+        for z, (more, less) in layers:
+            for h in range(2):
+                for ref, value in ((yp, more[h]), (ym, less[h])):
+                    ref[h, z, 4:8] = value[0:4]
+                    ref[h, z, 40:44] = value[4:8]
+        return carry
+
+    lax.fori_loop(0, nz // BLOCK, moved_rim, 0)
 
     for di, dj, copy in s_copies:
         @pl.when(inside(-di, -dj))
@@ -282,7 +353,9 @@
 
     for zp in range(zp_count):
         for r in WIDE:
-            own, left, right = (s[zp, r:r + 8] for s in (s_own, s_left, s_right))
+            own, left, right = s_own[zp, r:r + 8], s_left[zp // 2, r:r + 8], s_right[zp // 2, r:r + 8]
+            if zp % 2:
+                left, right = roll(left, -4), roll(right, 4)
             moved = roll(jnp.where(l16 < 12, left, own), -8)
             b0[zp, r:r + 8] = jnp.where(l16 < 8, moved, jnp.where(l16 < 12, own, right))
             moved = roll(jnp.where(l16 < 4, own, right), 8)
@@ -326,51 +399,6 @@
                     keep = jnp.logical_and(keep, keep_bottom)
                 strips[k + 1][zp, r:r + 8] = jnp.where(keep, total, 0.0)
 
-    for step, group in x_copies:
-        @pl.when(inside(-step, 0))
-        def _():
-            for copy in group:
-                copy.wait_recv()
-
-    def invert_rim(step, carry):
-        for u in range(BLOCK):
-            z = BLOCK * step + u
-            for h in range(2):
-                both = jnp.exp(-jnp.where(sub < 4, lp[h, z, 4:12], lp[h, z, 36:44]))
-                w[h, z, 4:8] = both[0:4]
-                w[h, z, 40:44] = both[4:8]
-        return carry
-
-    lax.fori_loop(0, nz // BLOCK, invert_rim, 0)
-
-    def faces_rim(step, carry):
-        layers = []
-        for u in range(BLOCK):
-            z = BLOCK * step + u
-            mids = [jnp.where(sub < 4, w[h, z, 4:12], w[h, z, 35:43]) for h in range(2)]
-            edge = [jnp.where(sub < 4, v0[h, z, 4:12], v0[h, z, 36:44]) for h in range(2)]
-            layers.append((z, mids, shifted(mids), shifted(edge)))
-        for z, mids, (right, left), (more, less) in layers:
-            above = jnp.minimum(z + 1, nz - 1)
-            top = jnp.where(z < nz - 1, 2.0, 0.0)
-            for h, mid in enumerate(mids):
-                across = jnp.where(sub < 4, w[h, z, 5:13], w[h, z, 36:44])
-                higher = jnp.where(sub < 4, w[h, above, 4:12], w[h, above, 35:43])
-                for ref, value in (
-                    (tx, 2.0 / (mid + across)),
-                    (ty, 2.0 / (mid + right[h])),
-                    (tym, 2.0 / (mid + left[h])),
-                    (tz, top / (mid + higher)),
-                ):
-                    ref[h, z, 4:8] = value[0:4]
-                    ref[h, z, 39:43] = value[4:8]
-                for ref, value in ((yp, more[h]), (ym, less[h])):
-                    ref[h, z, 4:8] = value[0:4]
-                    ref[h, z, 40:44] = value[4:8]
-        return carry
-
-    lax.fori_loop(0, nz // BLOCK, faces_rim, 0)
-
     for di, dj, copy in s_copies:
         @pl.when(inside(di, dj))
         def _():
@@ -408,7 +436,8 @@
         turn = lax.rem(248 - 16 * (z // zp_count), 128)
         return roll(q[k, lax.rem(z, zp_count), r:r + 8], turn)
 
-    moments = []
+    row = jnp.zeros((8, 128), F32)
+    found = 0
     for k in range(4):
         src, dst = fields[k], fields[k + 1]
         tiles = WIDE if k < 3 else OWN
@@ -482,20 +511,19 @@
         if k < 3:
             for u in range(BLOCK):
                 settle(nz - BLOCK + u, spread(nz - BLOCK + u))
-        if k == 0:
-            moments.append(sums[2])
-        moments.extend(sums[:2])
-
-    row = jnp.zeros((8, 128), F32)
-    for n, part in enumerate(moments):
-        row = jnp.where(lane == n, jnp.sum(part, axis=1, keepdims=True), row)
+        for part in ([sums[2]] if k == 0 else []) + list(sums[:2]):
+            row = jnp.where(lane == found, jnp.sum(part, axis=1, keepdims=True), row)
+            found += 1
+
     row = jnp.sum(row, axis=0, keepdims=True)
 
     def exchange(value, slot, red, count, send, recv, where):
         send_row[slot:slot + 1, :] = value
         red[0:1, :] = value
         copies = []
-        for d in range(1, count):
+        far = (lambda d: -min(d, count - d)) if count == gx else (
+            lambda d: -min(d % 4, 4 - d % 4) - min(d // 4, 4 - d // 4))
+        for d in sorted(range(1, count), key=far):
             copies.append(pltpu.make_async_remote_copy(
                 src_ref=send_row.at[pl.ds(slot, 1), :],
                 dst_ref=red.at[pl.ds(count - d, 1), :],
@@ -620,7 +648,9 @@
             in_specs=[hbm] * 2,
             out_specs=[vmem] * 8,
             scratch_shapes=[pltpu.VMEM(field, F32)] * 2
-            + [pltpu.VMEM(strip, F32)] * 12
+            + [pltpu.VMEM(strip, F32)]
+            + [pltpu.VMEM((zp // 2, ROWS, 128), F32)] * 4
+            + [pltpu.VMEM(strip, F32)] * 9
             + [pltpu.SemaphoreType.DMA((4,))]
             + [pltpu.SemaphoreType.DMA((8,))] * 4,
             compiler_params=pltpu.CompilerParams(

time: 34.5 us -> 33.3 us (0.965)
  Pallas kernels: 33.7 us -> 32.6 us
    pallas_call x1, Pallas kernels: 9.31 us -> 7.83 us  [on_device(): pl.pallas_call(functools.partial(gather, nz, gx, gy), out_shape=[pltpu.VM...]
where the time goes in v3:
time: 33.3 us; the launch traced here: 33.2 us
  Pallas kernels  32.6 us (98%)
  between operations  0.65 us (2%)
    pallas_call x1, Pallas kernels, on_device(): pl.pallas_call(functools.partial(powers, nz, gx, gy), out_shape=[pltpu.VM...  22.3 us
    pallas_call x1, Pallas kernels, on_device(): pl.pallas_call(functools.partial(gather, nz, gx, gy), out_shape=[pltpu.VM...  7.83 us
    pallas_call x1, Pallas kernels, on_device(): pl.pallas_call(functools.partial(finish, nz), out_shape=[shape] * 4, in_s...  2.41 us

profile of v3, /device:TPU:0, one launch (start us, length us, event | category | flops | bytes accessed | tf_op | source)
XLA Modules:
  0.0 33.2 jit_solution(17760659217152110972)
XLA Ops:
  0.6 7.8 %gather.1 = (f32[2,32,48,128]{3,2,1,0:T(8,128)S(1)}, f32[2,32,48,128]{3,2,1,0:T(8,128)S(1)}, f32[2,32,48,128]{3,2,1,0:T(8,128)S(1)}, f32[2,32,48,128]{3,2,1,0:T(...) custom-call(f32[1,32,32,256]{3,2,1,0:T(8,128)} %lp_ref.1, ...), custom_call_target="tpu_custom_call" | custom-call | tf_op jit(solution)/shard_map/gather/pallas_call | solution.py:645
  8.5 22.3 %powers.1 = (f32[2,32,48,128]{3,2,1,0:T(8,128)S(1)}, f32[2,32,48,128]{3,2,1,0:T(8,128)S(1)}, f32[2,32,48,128]{3,2,1,0:T(8,128)S(1)}, f32[2,32,48,128]{3,2,1,0:T(8,128)S(1)}, f32[4,8,128]{2,1,0:T(8,128)S(1)}) custom-call(f32[2,32,48,128]{3,2,1,0:T(8,128)S(1)} %get-tuple-element.17.v0, f32[2,32,48,128]{3,2,1,0:T(8,128)S(1)} %get-tuple-element.18.tx, ...), custom_call_target="tpu_custom_call" | custom-call | tf_op jit(solution)/shard_map/powers/pallas_call | solution.py:662
  30.8 2.4 %finish.1 = (f32[1,32,32,256]{3,2,1,0:T(8,128)}, f32[1,32,32,256]{3,2,1,0:T(8,128)}, f32[1,32,32,256]{3,2,1,0:T(8,128)}, f32[1,32,32,256]{3,2,1,0:T(8,128)}) custom-call(f32[2,32,48,128]{3,2,1,0:T(8,128)S(1)} %get-tuple-element.17.v0, f32[2,32,48,128]{3,2,1,0:T(8,128)S(1)} %get-tuple-element.25.v1, f32[2,32,48,128]{3,2,1,0:T(8,128)S(1)} %get-tuple-element.26.v2, ...), custom_call_target="tpu_custom_call" | custom-call | tf_op jit(solution)/shard_map/finish/pallas_call | solution.py:682

commit v4 on v3

--- a/solution.py
+++ b/solution.py
@@ -62,9 +62,12 @@
 
 def pair_div(x, y):
     q = x[0] / y[0]
-    zero = jnp.zeros_like(q)
-    rest = pair_add(x, neg(pair_mul(y, (q, zero))))
-    return quick(q, rest[0] / y[0])
+    p = q * y[0]
+    qh, ql = halves(q)
+    yh, yl = halves(y[0])
+    e = ((qh * yh - p) + qh * yl + ql * yh) + ql * yl
+    rest = ((x[0] - p) - (e + q * y[1])) + x[1]
+    return quick(q, rest / y[0])
 
 
 def coefficients(moments):
@@ -105,6 +108,11 @@
     right[0] = jnp.where(lane == 127, right[1], right[0])
     left[1] = jnp.where(lane == 0, left[0], left[1])
     return right, left
+
+
+def edges(strip, zp_count, step, u, r):
+    group = step * (BLOCK // zp_count) + u // zp_count
+    return roll(strip[u % zp_count, r:r + 8], 120 - 16 * group)
 
 
 def tree(hi, lo):
@@ -387,6 +395,8 @@
                 fy = tys[zp, r:r + 8] * (mid - roll(mid, -1))
                 q[k, zp, r:r + 8] = jnp.where(l16 == 8, roll(fy, 5), roll(fy, -4))
                 if k == 3:
+                    work = fy * (mid - roll(mid, -1))
+                    q[4, zp, r:r + 8] = jnp.where(l16 == 8, roll(work, 5), roll(work, -4))
                     continue
                 below = fzs[zp - 1, r:r + 8] if zp else roll(fzs[zp_count - 1, r:r + 8], 16)
                 total = txs[zp, r:r + 8] * (mid - field[zp, r + 1:r + 9])
@@ -421,10 +431,13 @@
     keep_bottom = jnp.logical_or(sub < 4, i < gx - 1)
 
     barrier = pltpu.get_barrier_semaphore()
-    for d in range(1, gx):
-        pl.semaphore_signal(barrier, inc=1, device_id=(lax.rem(i + d, gx), j), device_id_type=MESH)
-    for d in range(1, gy):
-        pl.semaphore_signal(barrier, inc=1, device_id=(i, lax.rem(j + d, gy)), device_id_type=MESH)
+
+    def greet():
+        for d in range(1, gx):
+            pl.semaphore_signal(barrier, inc=1, device_id=(lax.rem(i + d, gx), j), device_id_type=MESH)
+        for d in range(1, gy):
+            pl.semaphore_signal(barrier, inc=1, device_id=(i, lax.rem(j + d, gy)), device_id_type=MESH)
+
     for n, red in ((gx, red_a), (gy, red_b)):
         for r in range(n, red.shape[0]):
             red[r:r + 1, :] = jnp.zeros((1, 128), F32)
@@ -432,18 +445,16 @@
 
     steps = nz // BLOCK
 
-    def turned(k, z, r):
-        turn = lax.rem(248 - 16 * (z // zp_count), 128)
-        return roll(q[k, lax.rem(z, zp_count), r:r + 8], turn)
+    def turned(k, step, u, r):
+        return edges(q.at[k], zp_count, step, u, r)
 
     row = jnp.zeros((8, 128), F32)
     found = 0
-    for k in range(4):
-        src, dst = fields[k], fields[k + 1]
-        tiles = WIDE if k < 3 else OWN
+    for k in range(3):
+        src, dst, tiles = fields[k], fields[k + 1], WIDE
         for u in range(BLOCK):
             for n, r in enumerate(tiles):
-                sides[0, u, n] = turned(k, u, r)
+                sides[0, u, n] = turned(k, 0, u, r)
 
         def spread(z, dst=dst):
             return [shifted([dst[h, z, r:r + 8] for h in range(2)]) for r in WIDE]
@@ -453,20 +464,20 @@
             for r, (right, left) in zip(WIDE, moved):
                 for h in range(2):
                     yp[h, z, r:r + 8] = right[h]
-                    ym[h, z, r:r + 8] = left[h]
+                    if k < 2:
+                        ym[h, z, r:r + 8] = left[h]
 
         def block(step, carry, k=k, src=src, dst=dst, tiles=tiles, spread=spread, settle=settle):
             sums, below = list(carry[0]), list(carry[1])
-            after, before = ((yp0, ym0), (yp1, ym1), (yp2, ym2), (yp1, ym1))[k]
+            after, before = ((yp0, ym0), (yp1, ym1), (yp2, ym2))[k]
             now = lax.rem(step, 2)
+            coming = jnp.minimum(step + 1, steps - 1)
             moved = {}
             for u in range(BLOCK):
                 z = BLOCK * step + u
                 last = jnp.maximum(z - BLOCK, u)
-                later = jnp.minimum(z + BLOCK, nz - BLOCK + u)
-                if k < 3:
-                    moved = spread(last)
-                fresh = [turned(k, later, r) for r in tiles]
+                moved = spread(last)
+                fresh = [turned(k, coming, u, r) for r in tiles]
                 above = jnp.minimum(z + 1, nz - 1)
                 for n, r in enumerate(tiles):
                     rows, up, down = slice(r, r + 8), slice(r + 1, r + 9), slice(r - 1, r + 7)
@@ -497,27 +508,96 @@
                         if k == 0:
                             sums[2] = sums[2] + mine * mine
                         sums[0] = sums[0] + mine * new
-                        if k < 3:
-                            sums[1] = sums[1] + new * new
+                        sums[1] = sums[1] + new * new
                 for n in range(len(tiles)):
                     sides[1 - now, u, n] = fresh[n]
-                if k < 3:
-                    settle(last, moved)
+                settle(last, moved)
             return tuple(sums), tuple(below)
 
         zero = jnp.zeros((8, 128), F32)
-        count = 3 if k == 0 else 2 if k < 3 else 1
+        count = 2 if k else 3
         sums, _ = lax.fori_loop(0, steps, block, ((zero,) * count, (zero,) * (2 * len(tiles))))
-        if k < 3:
-            for u in range(BLOCK):
-                settle(nz - BLOCK + u, spread(nz - BLOCK + u))
+        for u in range(BLOCK):
+            settle(nz - BLOCK + u, spread(nz - BLOCK + u))
+        if k == 0:
+            greet()
         for part in ([sums[2]] if k == 0 else []) + list(sums[:2]):
             row = jnp.where(lane == found, jnp.sum(part, axis=1, keepdims=True), row)
             found += 1
 
+    for u in range(BLOCK):
+        for n, r in enumerate(OWN):
+            sides[0, u, n] = turned(4, 0, u, r)
+    first_row = jnp.logical_and(sub == 0, i == 0)
+    first_col = jnp.logical_and(lane == 0, j == 0)
+
+    def energy(step, carry):
+        acc = list(carry)
+        now = lax.rem(step, 2)
+        coming = jnp.minimum(step + 1, steps - 1)
+        for u in range(BLOCK):
+            z = BLOCK * step + u
+            fresh = [turned(4, coming, u, r) for r in OWN]
+            above = jnp.minimum(z + 1, nz - 1)
+            for n, r in enumerate(OWN):
+                rows, up, down = slice(r, r + 8), slice(r + 1, r + 9), slice(r - 1, r + 7)
+                side = sides[now, u, n]
+                for h in range(2):
+                    v = v3[h, z, rows]
+                    dx, dy, dz = v - v3[h, z, up], v - yp1[h, z, rows], v - v3[h, above, rows]
+                    across = ty[h, z, rows] * dy * dy
+                    if h == 0:
+                        acc[n] = acc[n] + jnp.where(first_col, side, 0.0)
+                    else:
+                        across = jnp.where(lane == 127, side, across)
+                    if r == OWN[0]:
+                        dm = v - v3[h, z, down]
+                        acc[h + 1] = acc[h + 1] + jnp.where(first_row, tx[h, z, down] * dm * dm, 0.0)
+                    term = tx[h, z, rows] * dx * dx + (across + tz[h, z, rows] * dz * dz)
+                    acc[4 * h + n] = acc[4 * h + n] + term
+            for n in range(len(OWN)):
+                sides[1 - now, u, n] = fresh[n]
+        return tuple(acc)
+
+    zero = jnp.zeros((8, 128), F32)
+    acc = lax.fori_loop(0, steps, energy, (zero,) * 8)
+    part = ((acc[0] + acc[1]) + (acc[2] + acc[3])) + ((acc[4] + acc[5]) + (acc[6] + acc[7]))
+    row = jnp.where(lane == found, jnp.sum(part, axis=1, keepdims=True), row)
     row = jnp.sum(row, axis=0, keepdims=True)
 
-    def exchange(value, slot, red, count, send, recv, where):
+    def fourth():
+        def block(step, below):
+            below, shifts = list(below), {}
+            for u in range(BLOCK):
+                z = BLOCK * step + u
+                for n, r in enumerate(OWN):
+                    left = [roll(v3[h, z, r:r + 8], 1) for h in range(2)]
+                    shifts[u, n] = (left[0], jnp.where(lane == 0, left[0], left[1]), turned(3, step, u, r))
+            for u in range(BLOCK):
+                z = BLOCK * step + u
+                above = jnp.minimum(z + 1, nz - 1)
+                for n, r in enumerate(OWN):
+                    rows, up, down = slice(r, r + 8), slice(r + 1, r + 9), slice(r - 1, r + 7)
+                    side = shifts[u, n][2]
+                    for h in range(2):
+                        v = v3[h, z, rows]
+                        ahead = ty[h, z, rows] * (v - yp1[h, z, rows])
+                        back = tym[h, z, rows] * (v - shifts[u, n][h])
+                        if h == 0:
+                            back = jnp.where(lane == 0, -side, back)
+                        else:
+                            ahead = jnp.where(lane == 127, side, ahead)
+                        fz = tz[h, z, rows] * (v - v3[h, above, rows])
+                        total = tx[h, z, rows] * (v - v3[h, z, up])
+                        total = total + tx[h, z, down] * (v - v3[h, z, down])
+                        v4[h, z, rows] = total + (ahead + back) + (fz - below[2 * n + h])
+                        below[2 * n + h] = fz
+            return tuple(below)
+
+        lax.fori_loop(0, steps, block, (zero,) * (2 * len(OWN)))
+
+
+    def exchange(value, slot, red, count, send, recv, where, meanwhile=None):
         send_row[slot:slot + 1, :] = value
         red[0:1, :] = value
         copies = []
@@ -534,12 +614,14 @@
             ))
         for copy in copies:
             copy.start()
+        if meanwhile is not None:
+            meanwhile()
         for copy in copies:
             copy.wait_recv()
         return copies
 
     pl.semaphore_wait(barrier, gx - 1 + gy - 1)
-    sent = exchange(row, 0, red_a, gx, a_send, a_recv, lambda d: (lax.rem(i + d, gx), j))
+    sent = exchange(row, 0, red_a, gx, a_send, a_recv, lambda d: (lax.rem(i + d, gx), j), fourth)
     part = red_a[...]
     hi, lo = tree(part, jnp.zeros_like(part))
     row = jnp.where(lane < 8, hi, pltpu.roll(lo, 8, 1))[0:1]
@@ -582,7 +664,6 @@
 
         def first(u):
             z = BLOCK * step + u
-            turn = lax.rem(248 - 16 * (z // zp_count), 128)
             for r in OWN:
                 press = []
                 for h in range(2):
@@ -593,7 +674,7 @@
                     p_buf[z, r - 8:r, cols] = press[h]
                     r_buf[z, r - 8:r, cols] = v[0] - combine(v[1:] + [v4[h, z, r:r + 8]])
                 moved[u, r] = [roll(p, -1) for p in press]
-                moved[u, r].append(roll(side[lax.rem(z, zp_count), r:r + 8], turn))
+                moved[u, r].append(edges(side, zp_count, step, u, r))
             for h in range(2):
                 wide[u, h, 40:48] = combine([f[h, z, 40:48] for f in (v0, v1, v2, v3)])
 
@@ -644,7 +725,7 @@
         hbm = pl.BlockSpec(memory_space=pltpu.HBM)
         made = pl.pallas_call(
             functools.partial(gather, nz, gx, gy),
-            out_shape=[pltpu.VMEM(field, F32)] * 7 + [pltpu.VMEM((4,) + strip, F32)],
+            out_shape=[pltpu.VMEM(field, F32)] * 7 + [pltpu.VMEM((5,) + strip, F32)],
             in_specs=[hbm] * 2,
             out_specs=[vmem] * 8,
             scratch_shapes=[pltpu.VMEM(field, F32)] * 2

time: 33.3 us -> 32.8 us (0.985)
  Pallas kernels: 32.6 us -> 32 us
    pallas_call x1, Pallas kernels: 22.3 us -> 21.8 us  [on_device(): pl.pallas_call(functools.partial(powers, nz, gx, gy), out_shape=[pltpu.VM...]
where the time goes in v4:
time: 32.8 us; the launch traced here: 32.7 us
  Pallas kernels  32 us (98%)
  between operations  0.65 us (2%)
    pallas_call x1, Pallas kernels, on_device(): pl.pallas_call(functools.partial(powers, nz, gx, gy), out_shape=[pltpu.VM...  21.8 us
    pallas_call x1, Pallas kernels, on_device(): pl.pallas_call(functools.partial(gather, nz, gx, gy), out_shape=[pltpu.VM...  7.87 us
    pallas_call x1, Pallas kernels, on_device(): pl.pallas_call(functools.partial(finish, nz), out_shape=[shape] * 4, in_s...  2.4 us

profile of v4, /device:TPU:0, one launch (start us, length us, event | category | flops | bytes accessed | tf_op | source)
XLA Modules:
  0.0 32.7 jit_solution(5732408811835646472)
XLA Ops:
  0.6 7.9 %gather.1 = (f32[2,32,48,128]{3,2,1,0:T(8,128)S(1)}, f32[2,32,48,128]{3,2,1,0:T(8,128)S(1)}, f32[2,32,48,128]{3,2,1,0:T(8,128)S(1)}, f32[2,32,48,128]{3,2,1,0:T(...) custom-call(f32[1,32,32,256]{3,2,1,0:T(8,128)} %lp_ref.1, ...), custom_call_target="tpu_custom_call" | custom-call | tf_op jit(solution)/shard_map/gather/pallas_call | solution.py:726
  8.5 21.8 %powers.1 = (f32[2,32,48,128]{3,2,1,0:T(8,128)S(1)}, f32[2,32,48,128]{3,2,1,0:T(8,128)S(1)}, f32[2,32,48,128]{3,2,1,0:T(8,128)S(1)}, f32[2,32,48,128]{3,2,1,0:T(8,128)S(1)}, f32[4,8,128]{2,1,0:T(8,128)S(1)}) custom-call(f32[2,32,48,128]{3,2,1,0:T(8,128)S(1)} %get-tuple-element.17.v0, f32[2,32,48,128]{3,2,1,0:T(8,128)S(1)} %get-tuple-element.18.tx, ...), custom_call_target="tpu_custom_call" | custom-call | tf_op jit(solution)/shard_map/powers/pallas_call | solution.py:743
  30.3 2.4 %finish.1 = (f32[1,32,32,256]{3,2,1,0:T(8,128)}, f32[1,32,32,256]{3,2,1,0:T(8,128)}, f32[1,32,32,256]{3,2,1,0:T(8,128)}, f32[1,32,32,256]{3,2,1,0:T(8,128)}) custom-call(f32[2,32,48,128]{3,2,1,0:T(8,128)S(1)} %get-tuple-element.17.v0, f32[2,32,48,128]{3,2,1,0:T(8,128)S(1)} %get-tuple-element.25.v1, f32[2,32,48,128]{3,2,1,0:T(8,128)S(1)} %get-tuple-element.26.v2, ...), custom_call_target="tpu_custom_call" | custom-call | tf_op jit(solution)/shard_map/finish/pallas_call | solution.py:763

commit v5 on v4

--- a/solution.py
+++ b/solution.py
@@ -14,7 +14,7 @@
 WIDE = (4, 12, 20, 28, 36)
 OWN = (8, 16, 24, 32)
 PARTS = 4
-BLOCK = 4
+BLOCK = 8
 DIRS = ((0, 1), (0, -1), (1, 0), (-1, 0), (1, 1), (1, -1), (-1, 1), (-1, -1))
 
 

time: 32.8 us -> 32.2 us (0.982)
  Pallas kernels: 32 us -> 31.5 us
    pallas_call x1, Pallas kernels: 21.8 us -> 21.3 us  [on_device(): pl.pallas_call(functools.partial(powers, nz, gx, gy), out_shape=[pltpu.VM...]
where the time goes in v5:
time: 32.2 us; the launch traced here: 32.1 us
  Pallas kernels  31.5 us (98%)
  between operations  0.65 us (2%)
    pallas_call x1, Pallas kernels, on_device(): pl.pallas_call(functools.partial(powers, nz, gx, gy), out_shape=[pltpu.VM...  21.3 us
    pallas_call x1, Pallas kernels, on_device(): pl.pallas_call(functools.partial(gather, nz, gx, gy), out_shape=[pltpu.VM...  7.87 us
    pallas_call x1, Pallas kernels, on_device(): pl.pallas_call(functools.partial(finish, nz), out_shape=[shape] * 4, in_s...  2.32 us

profile of v5, /device:TPU:0, one launch (start us, length us, event | category | flops | bytes accessed | tf_op | source)
XLA Modules:
  0.0 32.1 jit_solution(9419307648335952904)
XLA Ops:
  0.6 7.9 %gather.1 = (f32[2,32,48,128]{3,2,1,0:T(8,128)S(1)}, f32[2,32,48,128]{3,2,1,0:T(8,128)S(1)}, f32[2,32,48,128]{3,2,1,0:T(8,128)S(1)}, f32[2,32,48,128]{3,2,1,0:T(...) custom-call(f32[1,32,32,256]{3,2,1,0:T(8,128)} %lp_ref.1, ...), custom_call_target="tpu_custom_call" | custom-call | tf_op jit(solution)/shard_map/gather/pallas_call | solution.py:726
  8.5 21.3 %powers.1 = (f32[2,32,48,128]{3,2,1,0:T(8,128)S(1)}, f32[2,32,48,128]{3,2,1,0:T(8,128)S(1)}, f32[2,32,48,128]{3,2,1,0:T(8,128)S(1)}, f32[2,32,48,128]{3,2,1,0:T(8,128)S(1)}, f32[4,8,128]{2,1,0:T(8,128)S(1)}) custom-call(f32[2,32,48,128]{3,2,1,0:T(8,128)S(1)} %get-tuple-element.17.v0, f32[2,32,48,128]{3,2,1,0:T(8,128)S(1)} %get-tuple-element.18.tx, ...), custom_call_target="tpu_custom_call" | custom-call | tf_op jit(solution)/shard_map/powers/pallas_call | solution.py:743
  29.8 2.3 %finish.1 = (f32[1,32,32,256]{3,2,1,0:T(8,128)}, f32[1,32,32,256]{3,2,1,0:T(8,128)}, f32[1,32,32,256]{3,2,1,0:T(8,128)}, f32[1,32,32,256]{3,2,1,0:T(8,128)}) custom-call(f32[2,32,48,128]{3,2,1,0:T(8,128)S(1)} %get-tuple-element.17.v0, f32[2,32,48,128]{3,2,1,0:T(8,128)S(1)} %get-tuple-element.25.v1, f32[2,32,48,128]{3,2,1,0:T(8,128)S(1)} %get-tuple-element.26.v2, ...), custom_call_target="tpu_custom_call" | custom-call | tf_op jit(solution)/shard_map/finish/pallas_call | solution.py:763
